TPU v7x, 256 devices: a whole 4x4x8 slice. The times are simulated.
256 devices in a mesh: wide: 16 (over x, y_lo, core), loop: 16 (over y_hi, z).
Axes of the slice: x: 4, y: 4 (y_hi: 2, y_lo: 2; y = y_hi * 2 + y_lo), z: 8, core: 2. Of those that a mesh axis runs over, the one named last changes fastest.
Arguments:
- query_grads: bfloat16 [65536, 16384], P('loop', 'wide'), may hold values from -6 to 6
- train_grads: bfloat16 [640, 16384], P('loop', 'wide'), may hold values from -0.046875 to 0.046875
- precond: bfloat16 [2048, 16384], P(None, 'wide'), may hold values from -3 to 3
Outputs:
- scores: float32 [65536, 640], P(('loop', 'wide'))
All inputs are finite; a program needn't handle non-finite values.
Results may differ from a plain program's by a relative error of at most 0.0029.
Values may be sent and summed in bfloat16 or wider, within the bound.
No kernel may reach another device: no remote copies, remote signals or barrier semaphores. Data moves between devices by JAX's collectives and lax.ppermute only.
A program may use at most 128 MiB of HBM per device.

v0:
```python
import jax
import jax.numpy as jnp
from jax import lax
from jax.experimental import pallas as pl
from jax.experimental.pallas import tpu as pltpu
from jax.sharding import Mesh, PartitionSpec as P

DOT_NT = (((1,), (1,)), ((), ()))


def permute(block, axis, target):
    count = lax.axis_size(axis)
    return lax.ppermute(block, axis, [(i, target(i) % count) for i in range(count)])


def partial_scores_kernel(core_ref, own_rows_ref, mate_rows_ref, own_q_ref, mate_q_ref, out_ref):
    total = lax.dot_general(
        own_rows_ref[...], own_q_ref[...], DOT_NT, preferred_element_type=jnp.float32
    )
    total += lax.dot_general(
        mate_rows_ref[...], mate_q_ref[...], DOT_NT, preferred_element_type=jnp.float32
    )
    out_ref[...] = total.astype(jnp.bfloat16)[None]


def partial_scores(core, own_rows, mate_rows, own_q, mate_q, chips):
    rows, depth = own_rows.shape
    owned = own_q.shape[0] // (2 * chips)
    whole = pl.BlockSpec((rows, depth), lambda d, core_ref: (0, 0))
    queries = pl.BlockSpec((owned, depth), lambda d, core_ref: (2 * d + core_ref[0], 0))
    return pl.pallas_call(
        partial_scores_kernel,
        grid_spec=pltpu.PrefetchScalarGridSpec(
            num_scalar_prefetch=1,
            grid=(chips,),
            in_specs=[whole, whole, queries, queries],
            out_specs=pl.BlockSpec((1, rows, owned), lambda d, core_ref: (d, 0, 0)),
        ),
        out_shape=jax.ShapeDtypeStruct((chips, rows, owned), jnp.bfloat16),
        compiler_params=pltpu.CompilerParams(vmem_limit_bytes=56 * 2**20),
        cost_estimate=pl.CostEstimate(
            flops=4 * chips * owned * rows * depth,
            bytes_accessed=4 * chips * owned * depth + 4 * rows * depth + 2 * chips * owned * rows,
            transcendentals=0,
        ),
        name="partial_scores",
    )(core, own_rows, mate_rows, own_q, mate_q)


def total_scores_kernel(steps, block, z_ref, *refs):
    parts_refs, out_ref, placed_ref = refs[:-2], refs[-2], refs[-1]
    depth_z = sum(len(part) for part in steps)
    half = depth_z * block
    for parts_ref, part in zip(parts_refs, steps):
        for place, step in enumerate(part):
            z = lax.rem(z_ref[0] + step, depth_z)
            rows = pl.ds(place * 2 * block, 2 * block)
            total = parts_ref[0, rows, :].astype(jnp.float32)
            for chip in range(1, parts_ref.shape[0]):
                total += parts_ref[chip, rows, :].astype(jnp.float32)
            for side in range(2):
                first = pl.multiple_of(side * half + z * block, 8)
                placed_ref[pl.ds(first, block), :] = total[side * block : (side + 1) * block]
    out_ref[...] = placed_ref[...].T


def total_scores(z, parts, steps, block):
    owned = parts[0].shape[2]
    rows = sum(part.shape[1] for part in parts)
    return pl.pallas_call(
        lambda *refs: total_scores_kernel(steps, block, *refs),
        grid_spec=pltpu.PrefetchScalarGridSpec(
            num_scalar_prefetch=1,
            grid=(1,),
            in_specs=[pl.BlockSpec(part.shape, lambda i, z_ref: (0, 0, 0)) for part in parts],
            out_specs=pl.BlockSpec((owned, rows), lambda i, z_ref: (0, 0)),
            scratch_shapes=[pltpu.VMEM((rows, owned), jnp.float32)],
        ),
        out_shape=jax.ShapeDtypeStruct((owned, rows), jnp.float32),
        compiler_params=pltpu.CompilerParams(vmem_limit_bytes=32 * 2**20),
        cost_estimate=pl.CostEstimate(
            flops=8 * rows * owned, bytes_accessed=20 * rows * owned, transcendentals=0
        ),
        name="total_scores",
    )(z, *parts)


def shards(query_grads, train_grads, precond):
    core, y_hi, z = lax.axis_index("core"), lax.axis_index("y_hi"), lax.axis_index("z")

    def other_core(block):
        return permute(block, "core", lambda i: 1 - i)

    def scores_of(rows):
        parts = partial_scores(
            core.reshape(1), rows, other_core(rows), query_grads, query_mate, chips
        )
        return lax.all_to_all(parts, ("x", "y_lo"), split_axis=0, concat_axis=0, tiled=True)

    chips = lax.axis_size("x") * lax.axis_size("y_lo")
    train_mate = other_core(train_grads)
    query_sent, train_mate = lax.optimization_barrier((query_grads, train_mate))
    query_mate = other_core(query_sent)
    train_block = jnp.where(
        core == 1,
        jnp.concatenate([train_mate, train_grads], axis=1),
        jnp.concatenate([train_grads, train_mate], axis=1),
    )
    own = jnp.dot(train_block, precond, preferred_element_type=jnp.float32).astype(jnp.bfloat16)

    far = permute(own, "y_hi", lambda i: 1 - i)
    here = jnp.where(y_hi == 1, jnp.concatenate([far, own]), jnp.concatenate([own, far]))
    ahead1 = permute(here, "z", lambda i: i - 1)
    behind1 = permute(here, "z", lambda i: i + 1)
    across = permute(here, "z", lambda i: i + 4)
    ahead = permute(jnp.concatenate([ahead1, across]), "z", lambda i: i - 1)
    behind = permute(jnp.concatenate([across, behind1]), "z", lambda i: i + 1)
    near_parts = scores_of(jnp.concatenate([here, ahead1, across, behind1]))
    rest_parts = scores_of(jnp.concatenate([ahead, behind]))
    steps = ((0, 1, 4, 7), (2, 5, 3, 6))
    return total_scores(z.reshape(1), (near_parts, rest_parts), steps, own.shape[0])


def solution(mesh):
    split = Mesh(mesh.devices.reshape(4, 2, 2, 2, 8), ("x", "y_lo", "core", "y_hi", "z"))
    wide, loop = ("x", "y_lo", "core"), ("y_hi", "z")
    return jax.shard_map(
        shards,
        mesh=split,
        in_specs=(P(loop, wide), P(loop, wide), P(None, wide)),
        out_specs=P(loop + wide, None),
        check_vma=False,
    )
```

profile of v0, /device:TPU:1, one launch (start us, length us, event | category | flops | bytes accessed | tf_op | source)
XLA Modules:
  0.0 93.1 jit_solution(6849662267493353794)
XLA Ops:
  0.0 3.2 %collective-permute-start = (bf16[40,1024]{1,0:T(8,128)(2,1)}, bf16[40,1024]{1,0:T(8,128)(2,1)S(1)}, u32[]{:S(2)}, u32[]{:S(2)}) collective-permute-start(bf16[40,1024]{1,0:T(8,128)(2,1)} %param.4), channel_id=1, source_target_pairs={{0,16},{16,0},{1,17},{17,1},{2,18},{18,2},{3,19},{19,3},{4,20},{20... | collective-permute-start | bytes 245768 | tf_op jit(solution)/shard_map/ppermute | solution.py:13
  3.2 1.1 %collective-permute-done = bf16[40,1024]{1,0:T(8,128)(2,1)S(1)} collective-permute-done((bf16[40,1024]{1,0:T(8,128)(2,1)}, bf16[40,1024]{1,0:T(8,128)(2,1)S(1)}, u32[]{:S(2)}, u32[]{:S(2)}) %collective-permute-start) | collective-permute-done | bytes 81952 | tf_op jit(solution)/shard_map/ppermute | solution.py:13
  4.4 0.4 collective-permute-start.6
  4.7 3.1 %convolution_convert_fusion = bf16[40,1024]{1,0:T(8,128)(2,1)S(1)} fusion(bf16[2048,1024]{1,0:T(8,128)(2,1)} %param.5, bf16[40,1024]{1,0:T(8,128)(2,1)} %param.4, bf16[40,1024]{1,0:T(8,128)(2,1)S(1)} %collective-permute-done, pred[]{:T(512)S(6)} %eq.7), kind=kOutput, calls=%fused_computation | convolution fusion | flops 168550400 | bytes 4440065 | tf_op jit(solution)/shard_map/dot_general | solution.py:109
  7.8 1.3 %collective-permute-start.1 = (bf16[40,1024]{1,0:T(8,128)(2,1)S(1)}, bf16[40,1024]{1,0:T(8,128)(2,1)S(1)}, u32[]{:S(2)}, u32[]{:S(2)}) collective-permute-start(bf16[40,1024]{1,0:T(8,128)(2,1)S(1)} %convolution_convert_fusion), channel_id=1, source_target_pairs={{0,8},{8,0},{1,9},{9,1},{2,10},{10,2},{3,11},{11,3},{4,12},{12,4},... | collective-permute-start | bytes 245768 | tf_op jit(solution)/shard_map/ppermute | solution.py:13
  9.1 4.2 %collective-permute-done.1 = bf16[40,1024]{1,0:T(8,128)(2,1)S(1)} collective-permute-done((bf16[40,1024]{1,0:T(8,128)(2,1)S(1)}, bf16[40,1024]{1,0:T(8,128)(2,1)S(1)}, u32[]{:S(2)}, u32[]{:S(2)}) %collective-permute-start.1) | collective-permute-done | bytes 81952 | tf_op jit(solution)/shard_map/ppermute | solution.py:13
  13.4 0.1 collective-permute-start.4
  13.5 5.9 %collective-permute-start.3 = (bf16[80,1024]{1,0:T(8,128)(2,1)S(1)}, bf16[80,1024]{1,0:T(8,128)(2,1)S(1)}, u32[]{:S(2)}, u32[]{:S(2)}) collective-permute-start(bf16[80,1024]{1,0:T(8,128)(2,1)S(1)} %maximum_select_fusion.2), channel_id=1, source_target_pairs={{0,4},{1,5},{2,6},{3,7},{4,0},{5,1},{6,2},{7,3},{8,12},{9,13},{10,... | collective-permute-start | bytes 491528 | tf_op jit(solution)/shard_map/ppermute | solution.py:13
  19.4 1.9 %collective-permute-start.2 = (bf16[80,1024]{1,0:T(8,128)(2,1)S(1)}, bf16[80,1024]{1,0:T(8,128)(2,1)S(1)}, u32[]{:S(2)}, u32[]{:S(2)}) collective-permute-start(bf16[80,1024]{1,0:T(8,128)(2,1)S(1)} %maximum_select_fusion.2), channel_id=1, source_target_pairs={{0,7},{1,0},{2,1},{3,2},{4,3},{5,4},{6,5},{7,6},{8,15},{9,8},{10,9... | collective-permute-start | bytes 491528 | tf_op jit(solution)/shard_map/ppermute | solution.py:13
  21.3 0.0 collective-permute-done.4
  21.3 6.0 %collective-permute-done.3 = bf16[80,1024]{1,0:T(8,128)(2,1)S(1)} collective-permute-done((bf16[80,1024]{1,0:T(8,128)(2,1)S(1)}, bf16[80,1024]{1,0:T(8,128)(2,1)S(1)}, u32[]{:S(2)}, u32[]{:S(2)}) %collective-permute-start.3) | collective-permute-done | bytes 163872 | tf_op jit(solution)/shard_map/ppermute | solution.py:13
  27.3 2.9 %collective-permute-done.2 = bf16[80,1024]{1,0:T(8,128)(2,1)S(1)} collective-permute-done((bf16[80,1024]{1,0:T(8,128)(2,1)S(1)}, bf16[80,1024]{1,0:T(8,128)(2,1)S(1)}, u32[]{:S(2)}, u32[]{:S(2)}) %collective-permute-start.2) | collective-permute-done | bytes 163872 | tf_op jit(solution)/shard_map/ppermute | solution.py:13
  30.3 0.0 copy-start
  30.3 2.1 %collective-permute-start.5 = (bf16[320,1024]{1,0:T(8,128)(2,1)S(1)}, bf16[320,1024]{1,0:T(8,128)(2,1)S(1)}, u32[]{:S(2)}, u32[]{:S(2)}) collective-permute-start(bf16[320,1024]{1,0:T(8,128)(2,1)S(1)} %pad_maximum_fusion.own_rows_ref), channel_id=1, source_target_pairs={{0,16},{16,0},{1,17},{17,1},{2,18},{18,2},{3,19},{19,3},{4,20},{20... | collective-permute-start | bytes 1966088 | tf_op jit(solution)/shard_map/ppermute | solution.py:13
  32.4 0.1 pad_maximum_fusion.2
  32.5 2.5 %collective-permute-start.7 = (bf16[160,1024]{1,0:T(8,128)(2,1)S(1)}, bf16[160,1024]{1,0:T(8,128)(2,1)S(1)}, u32[]{:S(2)}, u32[]{:S(2)}) collective-permute-start(bf16[160,1024]{1,0:T(8,128)(2,1)S(1)} %get-tuple-element.10), channel_id=1, source_target_pairs={{0,7},{1,0},{2,1},{3,2},{4,3},{5,4},{6,5},{7,6},{8,15},{9,8},{10,9... | collective-permute-start | bytes 983048 | tf_op jit(solution)/shard_map/ppermute | solution.py:13
  35.0 0.0 collective-permute-start.8
  35.0 0.0 collective-permute-done.5.mate_rows_ref
  35.0 0.0 copy-start.2
  35.0 0.0 collective-permute-done.6.mate_q_ref
  35.0 0.0 copy-done
  35.0 0.8 copy-done.2
  35.8 9.1 %partial_scores.2 = bf16[8,320,256]{2,1,0:T(8,128)(2,1)} custom-call(s32[1]{0:T(128)} %bitcast.1.core_ref, bf16[320,1024]{1,0:T(8,128)(2,1)} %copy-done, bf16[320,1024]{1,0:T(8,128)(2,1)} %copy-done.2, bf16[4096,1024]{1,0:T(8,128)(2,1)} %own_q_ref.3, bf16[4096,1024]{1,0:T(8,128)(2,1)} %collective-permute-done.6.mate_q_ref), custom_call_target="tpu_custom_call" | custom-call | flops 2684354560 | bytes 11010048 | tf_op jit(solution)/shard_map/partial_scores/pallas_call | solution.py:31
  44.9 5.0 %all-to-all-start = ((bf16[8,320,256]{2,1,0:T(8,128)(2,1)}), bf16[8,320,256]{2,1,0:T(8,128)(2,1)S(1)}, u32[]{:S(2)}, u32[]{:S(2)}) async-start(bf16[8,320,256]{2,1,0:T(8,128)(2,1)} %partial_scores.2), calls=%async_computation | async-start | bytes 2621440 | tf_op jit(solution)/shard_map/all_to_all | solution.py:98
  49.9 0.0 collective-permute-done.7
  50.0 0.0 collective-permute-done.8
  50.0 0.0 copy-start.1
  50.0 0.7 collective-permute-start.9
  50.7 1.7 %collective-permute-done.9.mate_rows_ref = bf16[320,1024]{1,0:T(8,128)(2,1)S(1)} collective-permute-done((bf16[320,1024]{1,0:T(8,128)(2,1)S(1)}, bf16[320,1024]{1,0:T(8,128)(2,1)S(1)}, u32[]{:S(2)}, u32[]{:S(2)}) %collective-permute-start.9) | collective-permute-done | bytes 655392 | tf_op jit(solution)/shard_map/ppermute | solution.py:13
  52.4 0.0 copy-done.1
  52.4 0.0 copy-start.3
  52.4 0.8 copy-done.3
  53.2 9.1 %partial_scores.3 = bf16[8,320,256]{2,1,0:T(8,128)(2,1)} custom-call(s32[1]{0:T(128)} %bitcast.1.core_ref, bf16[320,1024]{1,0:T(8,128)(2,1)} %copy-done.1, bf16[320,1024]{1,0:T(8,128)(2,1)} %copy-done.3, bf16[4096,1024]{1,0:T(8,128)(2,1)} %own_q_ref.3, bf16[4096,1024]{1,0:T(8,128)(2,1)} %collective-permute-done.6.mate_q_ref), custom_call_target="tpu_custom_call" | custom-call | flops 2684354560 | bytes 11010048 | tf_op jit(solution)/shard_map/partial_scores/pallas_call | solution.py:31
  62.3 7.4 %all-to-all-done.refs_1_ = bf16[8,320,256]{2,1,0:T(8,128)(2,1)S(1)} async-done(((bf16[8,320,256]{2,1,0:T(8,128)(2,1)}), bf16[8,320,256]{2,1,0:T(8,128)(2,1)S(1)}, u32[]{:S(2)}, u32[]{:S(2)}) %all-to-all-start) | async-done | bytes 1310752 | tf_op jit(solution)/shard_map/all_to_all | solution.py:98
  69.7 3.6 %all-to-all-start.1 = ((bf16[8,320,256]{2,1,0:T(8,128)(2,1)}), bf16[8,320,256]{2,1,0:T(8,128)(2,1)S(1)}, u32[]{:S(2)}, u32[]{:S(2)}) async-start(bf16[8,320,256]{2,1,0:T(8,128)(2,1)} %partial_scores.3), calls=%async_computation.1 | async-start | bytes 2621440 | tf_op jit(solution)/shard_map/all_to_all | solution.py:98
  73.3 18.4 %all-to-all-done.1.refs_2_ = bf16[8,320,256]{2,1,0:T(8,128)(2,1)S(1)} async-done(((bf16[8,320,256]{2,1,0:T(8,128)(2,1)}), bf16[8,320,256]{2,1,0:T(8,128)(2,1)S(1)}, u32[]{:S(2)}, u32[]{:S(2)}) %all-to-all-start.1) | async-done | bytes 1310752 | tf_op jit(solution)/shard_map/all_to_all | solution.py:98
  91.7 1.4 %total_scores.1 = f32[256,640]{1,0:T(8,128)} custom-call(s32[1]{0:T(128)} %bitcast.refs_0_, bf16[8,320,256]{2,1,0:T(8,128)(2,1)S(1)} %all-to-all-done.refs_1_, bf16[8,320,256]{2,1,0:T(8,128)(2,1)S(1)} %all-to-all-done.1.refs_2_), custom_call_target="tpu_custom_call" | custom-call | flops 1310720 | bytes 3276800 | tf_op jit(solution)/shard_map/total_scores/pallas_call | solution.py:70
  (4 shorter events, 0.1 us)
Async XLA Ops:
  0.0 4.4 %collective-permute-start = (bf16[40,1024]{1,0:T(8,128)(2,1)}, bf16[40,1024]{1,0:T(8,128)(2,1)S(1)}, u32[]{:S(2)}, u32[]{:S(2)}) collective-permute-start(bf16[40,1024]{1,0:T(8,128)(2,1)} %param.4), channel_id=1, source_target_pairs={{0,16},{16,0},{1,17},{17,1},{2,18},{18,2},{3,19},{19,3},{4,20},{20... | collective-permute-start | bytes 245768 | tf_op jit(solution)/shard_map/ppermute | solution.py:13
  4.4 30.6 %collective-permute-start.6 = (bf16[4096,1024]{1,0:T(8,128)(2,1)}, bf16[4096,1024]{1,0:T(8,128)(2,1)}, u32[]{:S(2)}, u32[]{:S(2)}) collective-permute-start(bf16[4096,1024]{1,0:T(8,128)(2,1)} %own_q_ref.3), channel_id=1, source_target_pairs={{0,16},{16,0},{1,17},{17,1},{2,18},{18,2},{3,19},{19,3},{4,20},{20... | collective-permute-start | bytes 25165832 | tf_op jit(solution)/shard_map/ppermute | solution.py:13
  7.8 5.5 %collective-permute-start.1 = (bf16[40,1024]{1,0:T(8,128)(2,1)S(1)}, bf16[40,1024]{1,0:T(8,128)(2,1)S(1)}, u32[]{:S(2)}, u32[]{:S(2)}) collective-permute-start(bf16[40,1024]{1,0:T(8,128)(2,1)S(1)} %convolution_convert_fusion), channel_id=1, source_target_pairs={{0,8},{8,0},{1,9},{9,1},{2,10},{10,2},{3,11},{11,3},{4,12},{12,4},... | collective-permute-start | bytes 245768 | tf_op jit(solution)/shard_map/ppermute | solution.py:13
  13.4 7.9 %collective-permute-start.4 = (bf16[80,1024]{1,0:T(8,128)(2,1)S(1)}, bf16[80,1024]{1,0:T(8,128)(2,1)S(1)}, u32[]{:S(2)}, u32[]{:S(2)}) collective-permute-start(bf16[80,1024]{1,0:T(8,128)(2,1)S(1)} %maximum_select_fusion.2), channel_id=1, source_target_pairs={{0,1},{1,2},{2,3},{3,4},{4,5},{5,6},{6,7},{7,0},{8,9},{9,10},{10,1... | collective-permute-start | bytes 491528 | tf_op jit(solution)/shard_map/ppermute | solution.py:13
  13.5 13.9 %collective-permute-start.3 = (bf16[80,1024]{1,0:T(8,128)(2,1)S(1)}, bf16[80,1024]{1,0:T(8,128)(2,1)S(1)}, u32[]{:S(2)}, u32[]{:S(2)}) collective-permute-start(bf16[80,1024]{1,0:T(8,128)(2,1)S(1)} %maximum_select_fusion.2), channel_id=1, source_target_pairs={{0,4},{1,5},{2,6},{3,7},{4,0},{5,1},{6,2},{7,3},{8,12},{9,13},{10,... | collective-permute-start | bytes 491528 | tf_op jit(solution)/shard_map/ppermute | solution.py:13
  19.4 10.9 %collective-permute-start.2 = (bf16[80,1024]{1,0:T(8,128)(2,1)S(1)}, bf16[80,1024]{1,0:T(8,128)(2,1)S(1)}, u32[]{:S(2)}, u32[]{:S(2)}) collective-permute-start(bf16[80,1024]{1,0:T(8,128)(2,1)S(1)} %maximum_select_fusion.2), channel_id=1, source_target_pairs={{0,7},{1,0},{2,1},{3,2},{4,3},{5,4},{6,5},{7,6},{8,15},{9,8},{10,9... | collective-permute-start | bytes 491528 | tf_op jit(solution)/shard_map/ppermute | solution.py:13
  30.3 4.7 %copy-start = (bf16[320,1024]{1,0:T(8,128)(2,1)}, bf16[320,1024]{1,0:T(8,128)(2,1)S(1)}, u32[]{:S(2)}) copy-start(bf16[320,1024]{1,0:T(8,128)(2,1)S(1)} %pad_maximum_fusion.own_rows_ref) | copy-start | bytes 1966084
  30.3 4.7 %collective-permute-start.5 = (bf16[320,1024]{1,0:T(8,128)(2,1)S(1)}, bf16[320,1024]{1,0:T(8,128)(2,1)S(1)}, u32[]{:S(2)}, u32[]{:S(2)}) collective-permute-start(bf16[320,1024]{1,0:T(8,128)(2,1)S(1)} %pad_maximum_fusion.own_rows_ref), channel_id=1, source_target_pairs={{0,16},{16,0},{1,17},{17,1},{2,18},{18,2},{3,19},{19,3},{4,20},{20... | collective-permute-start | bytes 1966088 | tf_op jit(solution)/shard_map/ppermute | solution.py:13
  32.5 17.4 %collective-permute-start.7 = (bf16[160,1024]{1,0:T(8,128)(2,1)S(1)}, bf16[160,1024]{1,0:T(8,128)(2,1)S(1)}, u32[]{:S(2)}, u32[]{:S(2)}) collective-permute-start(bf16[160,1024]{1,0:T(8,128)(2,1)S(1)} %get-tuple-element.10), channel_id=1, source_target_pairs={{0,7},{1,0},{2,1},{3,2},{4,3},{5,4},{6,5},{7,6},{8,15},{9,8},{10,9... | collective-permute-start | bytes 983048 | tf_op jit(solution)/shard_map/ppermute | solution.py:13
  35.0 15.0 %collective-permute-start.8 = (bf16[160,1024]{1,0:T(8,128)(2,1)S(1)}, bf16[160,1024]{1,0:T(8,128)(2,1)S(1)}, u32[]{:S(2)}, u32[]{:S(2)}) collective-permute-start(bf16[160,1024]{1,0:T(8,128)(2,1)S(1)} %get-tuple-element.9), channel_id=1, source_target_pairs={{0,1},{1,2},{2,3},{3,4},{4,5},{5,6},{6,7},{7,0},{8,9},{9,10},{10,1... | collective-permute-start | bytes 983048 | tf_op jit(solution)/shard_map/ppermute | solution.py:13
  35.0 0.8 copy-start.2
  44.9 24.8 %all-to-all-start = ((bf16[8,320,256]{2,1,0:T(8,128)(2,1)}), bf16[8,320,256]{2,1,0:T(8,128)(2,1)S(1)}, u32[]{:S(2)}, u32[]{:S(2)}) async-start(bf16[8,320,256]{2,1,0:T(8,128)(2,1)} %partial_scores.2), calls=%async_computation | async-start | bytes 2621440 | tf_op jit(solution)/shard_map/all_to_all | solution.py:98
  50.0 2.4 %copy-start.1 = (bf16[320,1024]{1,0:T(8,128)(2,1)}, bf16[320,1024]{1,0:T(8,128)(2,1)S(1)}, u32[]{:S(2)}) copy-start(bf16[320,1024]{1,0:T(8,128)(2,1)S(1)} %constant_dynamic-update-slice_fusion.own_rows_ref) | copy-start | bytes 1966084
  50.0 2.4 %collective-permute-start.9 = (bf16[320,1024]{1,0:T(8,128)(2,1)S(1)}, bf16[320,1024]{1,0:T(8,128)(2,1)S(1)}, u32[]{:S(2)}, u32[]{:S(2)}) collective-permute-start(bf16[320,1024]{1,0:T(8,128)(2,1)S(1)} %constant_dynamic-update-slice_fusion.own_rows_ref), channel_id=1, source_target_pairs={{0,16},{16,0},{1,17},{17,1},{2,18},{18,2},{3,19},{19,3},{4,20},{20... | collective-permute-start | bytes 1966088 | tf_op jit(solution)/shard_map/ppermute | solution.py:13
  52.4 0.8 copy-start.3
  69.7 22.0 %all-to-all-start.1 = ((bf16[8,320,256]{2,1,0:T(8,128)(2,1)}), bf16[8,320,256]{2,1,0:T(8,128)(2,1)S(1)}, u32[]{:S(2)}, u32[]{:S(2)}) async-start(bf16[8,320,256]{2,1,0:T(8,128)(2,1)} %partial_scores.3), calls=%async_computation.1 | async-start | bytes 2621440 | tf_op jit(solution)/shard_map/all_to_all | solution.py:98
where the time goes:
time: 93.7 us; the launch traced here: 93.1 us
  waiting for transfers between devices  41.8 us (45%)
  starting transfers between devices  26.6 us (28%)
  Pallas kernels  19.6 us (21%)
  matrix products  3.11 us (3%)
  local copies, waits for them, and re-layouts  1.71 us (2%)
    all_to_all x2, waiting for transfers between devices, scores_of(): lax.all_to_all(parts, ('x', 'y_lo'), split_axis=0, concat_axis=0, tiled=T...  25.8 us
    pallas_call x2, Pallas kernels, partial_scores(): pl.pallas_call(partial_scores_kernel, grid_spec=pltpu.PrefetchScalarGridS...  18.2 us
    ppermute x10, starting transfers between devices, permute(): lax.ppermute(block, axis, [(i, target(i) % count) for i in range(count)])  18 us
    ppermute x10, waiting for transfers between devices, permute(): lax.ppermute(block, axis, [(i, target(i) % count) for i in range(count)])  16 us
    all_to_all x2, starting transfers between devices, scores_of(): lax.all_to_all(parts, ('x', 'y_lo'), split_axis=0, concat_axis=0, tiled=T...  8.6 us
    dot_general x1, matrix products, shards(): jnp.dot(train_block, precond, preferred_element_type=jnp.float32)  3.11 us
  transfers between devices with their start and end apart: 12, of which 7 were waited for; matrix products, arithmetic and copies ran while one was open for 4% of the time, Pallas kernels for 20%

commit v1 on v0

v1 whole, which is shorter than its diff:
```python
import jax
import jax.numpy as jnp
from jax import lax
from jax.experimental import pallas as pl
from jax.experimental.pallas import tpu as pltpu
from jax.sharding import Mesh, PartitionSpec as P

def permute(block, axis, target):
    count = lax.axis_size(axis)
    return lax.ppermute(block, axis, [(i, target(i) % count) for i in range(count)])


def scores_against(rows, queries):
    return lax.dot_general(
        rows, queries, (((1,), (1,)), ((), ())), preferred_element_type=jnp.float32
    )


def total_scores_kernel(steps, block, z_ref, *refs):
    chunk_refs, out_ref, placed_ref = refs[:-2], refs[-2], refs[-1]
    depth_z = sum(len(chunk) for chunk in steps)
    half = depth_z * block
    for index, chunk in enumerate(steps):
        count = len(chunk_refs) // len(steps)
        parts = chunk_refs[index * count : (index + 1) * count]
        for place, step in enumerate(chunk):
            z = lax.rem(z_ref[0] + step, depth_z)
            rows = pl.ds(place * 2 * block, 2 * block)
            total = parts[0][rows, :]
            for part in parts[1:]:
                total += part[rows, :].astype(jnp.float32)
            for side in range(2):
                first = pl.multiple_of(side * half + z * block, 8)
                placed_ref[pl.ds(first, block), :] = total[side * block : (side + 1) * block]
    out_ref[...] = placed_ref[...].T


def total_scores(z, chunks, steps, block):
    owned = chunks[0][0].shape[1]
    rows = sum(chunk[0].shape[0] for chunk in chunks)
    parts = [part for chunk in chunks for part in chunk]
    return pl.pallas_call(
        lambda *refs: total_scores_kernel(steps, block, *refs),
        grid_spec=pltpu.PrefetchScalarGridSpec(
            num_scalar_prefetch=1,
            grid=(1,),
            in_specs=[pl.BlockSpec(part.shape, lambda i, z_ref: (0, 0)) for part in parts],
            out_specs=pl.BlockSpec((owned, rows), lambda i, z_ref: (0, 0)),
            scratch_shapes=[pltpu.VMEM((rows, owned), jnp.float32)],
        ),
        out_shape=jax.ShapeDtypeStruct((owned, rows), jnp.float32),
        compiler_params=pltpu.CompilerParams(vmem_limit_bytes=16 * 2**20),
        cost_estimate=pl.CostEstimate(
            flops=8 * rows * owned, bytes_accessed=20 * rows * owned, transcendentals=0
        ),
        name="total_scores",
    )(z, *parts)


def shards(query_grads, train_grads, precond):
    core, y_hi, z = lax.axis_index("core"), lax.axis_index("y_hi"), lax.axis_index("z")

    def other_core(block):
        return permute(block, "core", lambda i: 1 - i)

    def scored_here(queries):
        by_owner = queries.reshape(count_x, count_y, 2, -1, queries.shape[1])
        blocks = []
        for step_x, step_y in owners:
            start = ((x + step_x) % count_x, (y_lo + step_y) % count_y, core, 0, 0)
            size = (1, 1, 1) + by_owner.shape[3:]
            blocks.append(lax.dynamic_slice(by_owner, start, size).reshape(size[3:]))
        return blocks

    def to_owner(part, step_x, step_y):
        route = []
        for i in range(count_x * count_y):
            to_x, to_y = (i // count_y + step_x) % count_x, (i % count_y + step_y) % count_y
            route.append((i, to_x * count_y + to_y))
        return lax.ppermute(part, ("x", "y_lo"), route)

    def totals_of(rows):
        mate_rows = other_core(rows)
        parts = []
        for (step_x, step_y), own_block, mate_block in zip(owners, own_q, mate_q):
            part = scores_against(rows, own_block) + scores_against(mate_rows, mate_block)
            if step_x or step_y:
                part = to_owner(part.astype(jnp.bfloat16), step_x, step_y)
            parts.append(part)
        return parts[-1:] + parts[:-1]

    count_x, count_y = lax.axis_size("x"), lax.axis_size("y_lo")
    x, y_lo = lax.axis_index("x"), lax.axis_index("y_lo")
    owners = [(2, 1), (1, 1), (3, 1), (2, 0), (0, 1), (1, 0), (3, 0), (0, 0)]
    train_mate = other_core(train_grads)
    query_sent, train_mate = lax.optimization_barrier((query_grads, train_mate))
    query_mate = other_core(query_sent)
    train_block = jnp.where(
        core == 1,
        jnp.concatenate([train_mate, train_grads], axis=1),
        jnp.concatenate([train_grads, train_mate], axis=1),
    )
    own = jnp.dot(train_block, precond, preferred_element_type=jnp.float32).astype(jnp.bfloat16)

    far = permute(own, "y_hi", lambda i: 1 - i)
    own_q = scored_here(lax.optimization_barrier((query_grads, own))[0])
    *own_q, far = lax.optimization_barrier((*own_q, far))
    here = jnp.where(y_hi == 1, jnp.concatenate([far, own]), jnp.concatenate([own, far]))
    ahead1 = permute(here, "z", lambda i: i - 1)
    behind1 = permute(here, "z", lambda i: i + 1)
    across = permute(here, "z", lambda i: i + 4)
    mate_q = scored_here(query_mate)
    *mate_q, ahead1 = lax.optimization_barrier((*mate_q, ahead1))
    ahead = permute(jnp.concatenate([ahead1, across]), "z", lambda i: i - 1)
    behind = permute(jnp.concatenate([across, behind1]), "z", lambda i: i + 1)
    near = totals_of(jnp.concatenate([here, ahead1, across, behind1]))
    near[1], ahead, behind = lax.optimization_barrier((near[1], ahead, behind))
    rest = totals_of(jnp.concatenate([ahead, behind]))
    steps = ((0, 1, 4, 7), (2, 5, 3, 6))
    return total_scores(z.reshape(1), (near, rest), steps, own.shape[0])


def solution(mesh):
    split = Mesh(mesh.devices.reshape(4, 2, 2, 2, 8), ("x", "y_lo", "core", "y_hi", "z"))
    wide, loop = ("x", "y_lo", "core"), ("y_hi", "z")
    return jax.shard_map(
        shards,
        mesh=split,
        in_specs=(P(loop, wide), P(loop, wide), P(None, wide)),
        out_specs=P(loop + wide, None),
        check_vma=False,
    )
```

time: 93.7 us -> 86.5 us (0.923)
  waiting for transfers between devices: 41.8 us -> 19.8 us
  Pallas kernels: 19.6 us -> 1.37 us
  matrix products: 3.11 us -> 15 us
  starting transfers between devices: 26.6 us -> 36 us
  local copies, waits for them, and re-layouts: 1.71 us -> 11 us
  other arithmetic: 0.14 us -> 2.12 us
    all_to_all x2 -> x0, waiting for transfers between devices: 25.8 us -> none  [scores_of(): lax.all_to_all(parts, ('x', 'y_lo'), split_axis=0, concat_axis=0, tiled=T...]
    pallas_call x2 -> x0, Pallas kernels: 18.2 us -> none  [partial_scores(): pl.pallas_call(partial_scores_kernel, grid_spec=pltpu.PrefetchScalarGridS...]
    ppermute x0 -> x14, starting transfers between devices: none -> 16.9 us  [to_owner(): return lax.ppermute(part, ('x', 'y_lo'), route)]
    ppermute x0 -> x14, waiting for transfers between devices: none -> 13.2 us  [to_owner(): return lax.ppermute(part, ('x', 'y_lo'), route)]
    dot_general x0 -> x32, matrix products: none -> 11.9 us  [scores_against(): lax.dot_general(rows, queries, (((1,), (1,)), ((), ())), preferred_elemen...]
    ppermute x10, waiting for transfers between devices: 16 us -> 6.62 us  [permute(): lax.ppermute(block, axis, [(i, target(i) % count) for i in range(count)])]
    all_to_all x2 -> x0, starting transfers between devices: 8.6 us -> none  [scores_of(): lax.all_to_all(parts, ('x', 'y_lo'), split_axis=0, concat_axis=0, tiled=T...]
    reshape x0 -> x2, local copies, waits for them, and re-layouts: none -> 7.95 us  [scored_here(): blocks.append(lax.dynamic_slice(by_owner, start, size).reshape(size[3:]))]
  transfers between devices with their start and end apart: 12 -> 24, of which waited for: 7 -> 7; matrix products, arithmetic and copies ran while one was open for 4% -> 28% of each run, Pallas kernels for 20% -> 0%
where the time goes in v1:
time: 86.5 us; the launch traced here: 85.7 us
  starting transfers between devices  36 us (42%)
  waiting for transfers between devices  19.8 us (23%)
  matrix products  15 us (17%)
  local copies, waits for them, and re-layouts  11 us (13%)
  other arithmetic  2.12 us (2%)
  Pallas kernels  1.37 us (2%)
    ppermute x10, starting transfers between devices, permute(): lax.ppermute(block, axis, [(i, target(i) % count) for i in range(count)])  19.1 us
    ppermute x14, starting transfers between devices, to_owner(): return lax.ppermute(part, ('x', 'y_lo'), route)  16.9 us
    ppermute x14, waiting for transfers between devices, to_owner(): return lax.ppermute(part, ('x', 'y_lo'), route)  13.2 us
    dot_general x32, matrix products, scores_against(): lax.dot_general(rows, queries, (((1,), (1,)), ((), ())), preferred_elemen...  11.9 us
    reshape x2, local copies, waits for them, and re-layouts, scored_here(): blocks.append(lax.dynamic_slice(by_owner, start, size).reshape(size[3:]))  7.95 us
    ppermute x10, waiting for transfers between devices, permute(): lax.ppermute(block, axis, [(i, target(i) % count) for i in range(count)])  6.62 us
    dot_general x1, matrix products, shards(): jnp.dot(train_block, precond, preferred_element_type=jnp.float32)  3.11 us
    unnamed x35, local copies, waits for them, and re-layouts  2.99 us
  transfers between devices with their start and end apart: 24, of which 7 were waited for; matrix products, arithmetic and copies ran while one was open for 28% of the time, Pallas kernels for 0%

profile of v1, /device:TPU:1, one launch (start us, length us, event | category | flops | bytes accessed | tf_op | source)
XLA Modules:
  0.0 85.7 jit_solution(14077691675458724999)
XLA Ops:
  0.0 3.2 %collective-permute-start = (bf16[40,1024]{1,0:T(8,128)(2,1)}, bf16[40,1024]{1,0:T(8,128)(2,1)S(1)}, u32[]{:S(2)}, u32[]{:S(2)}) collective-permute-start(bf16[40,1024]{1,0:T(8,128)(2,1)} %param.4), channel_id=1, source_target_pairs={{0,16},{16,0},{1,17},{17,1},{2,18},{18,2},{3,19},{19,3},{4,20},{20... | collective-permute-start | bytes 245768 | tf_op jit(solution)/shard_map/ppermute | solution.py:10
  3.2 1.1 %collective-permute-done = bf16[40,1024]{1,0:T(8,128)(2,1)S(1)} collective-permute-done((bf16[40,1024]{1,0:T(8,128)(2,1)}, bf16[40,1024]{1,0:T(8,128)(2,1)S(1)}, u32[]{:S(2)}, u32[]{:S(2)}) %collective-permute-start) | collective-permute-done | bytes 81952 | tf_op jit(solution)/shard_map/ppermute | solution.py:10
  4.7 3.1 %convolution_convert_fusion = bf16[40,1024]{1,0:T(8,128)(2,1)S(1)} fusion(bf16[2048,1024]{1,0:T(8,128)(2,1)} %param.5, bf16[40,1024]{1,0:T(8,128)(2,1)} %param.4, bf16[40,1024]{1,0:T(8,128)(2,1)S(1)} %collective-permute-done, pred[]{:T(512)S(6)} %eq.40), kind=kOutput, calls=%fused_computation.30 | convolution fusion | flops 168550400 | bytes 4440065 | tf_op jit(solution)/shard_map/dot_general | solution.py:103
  7.8 1.3 %collective-permute-start.1 = (bf16[40,1024]{1,0:T(8,128)(2,1)S(1)}, bf16[40,1024]{1,0:T(8,128)(2,1)S(1)}, u32[]{:S(2)}, u32[]{:S(2)}) collective-permute-start(bf16[40,1024]{1,0:T(8,128)(2,1)S(1)} %convolution_convert_fusion), channel_id=1, source_target_pairs={{0,8},{8,0},{1,9},{9,1},{2,10},{10,2},{3,11},{11,3},{4,12},{12,4},... | collective-permute-start | bytes 245768 | tf_op jit(solution)/shard_map/ppermute | solution.py:10
  9.1 4.2 %dynamic-slice_bitcast_fusion.8 = (bf16[256,1024]{1,0:T(8,128)(2,1)}, bf16[256,1024]{1,0:T(8,128)(2,1)}, bf16[256,1024]{1,0:T(8,128)(2,1)}, bf16[256,1024]{1,0:T...) fusion(bf16[4,2,2,256,1024]{4,3,2,1,0:T(8,128)(2,1)} %bitcast.9, ...), kind=kLoop, calls=%fused_computation.40 | loop fusion | bytes 8388636 | tf_op jit(solution)/shard_map/reshape | solution.py:72
  13.4 5.7 %collective-permute-start.3 = (bf16[80,1024]{1,0:T(8,128)(2,1)S(1)}, bf16[80,1024]{1,0:T(8,128)(2,1)S(1)}, u32[]{:S(2)}, u32[]{:S(2)}) collective-permute-start(bf16[80,1024]{1,0:T(8,128)(2,1)S(1)} %maximum_select_fusion.2), channel_id=1, source_target_pairs={{0,7},{1,0},{2,1},{3,2},{4,3},{5,4},{6,5},{7,6},{8,15},{9,8},{10,9... | collective-permute-start | bytes 491528 | tf_op jit(solution)/shard_map/ppermute | solution.py:10
  19.1 1.4 %collective-permute-start.4 = (bf16[80,1024]{1,0:T(8,128)(2,1)S(1)}, bf16[80,1024]{1,0:T(8,128)(2,1)S(1)}, u32[]{:S(2)}, u32[]{:S(2)}) collective-permute-start(bf16[80,1024]{1,0:T(8,128)(2,1)S(1)} %maximum_select_fusion.2), channel_id=1, source_target_pairs={{0,4},{1,5},{2,6},{3,7},{4,0},{5,1},{6,2},{7,3},{8,12},{9,13},{10,... | collective-permute-start | bytes 491528 | tf_op jit(solution)/shard_map/ppermute | solution.py:10
  20.5 1.4 %collective-permute-start.5 = (bf16[80,1024]{1,0:T(8,128)(2,1)S(1)}, bf16[80,1024]{1,0:T(8,128)(2,1)S(1)}, u32[]{:S(2)}, u32[]{:S(2)}) collective-permute-start(bf16[80,1024]{1,0:T(8,128)(2,1)S(1)} %maximum_select_fusion.2), channel_id=1, source_target_pairs={{0,1},{1,2},{2,3},{3,4},{4,5},{5,6},{6,7},{7,0},{8,9},{9,10},{10,1... | collective-permute-start | bytes 491528 | tf_op jit(solution)/shard_map/ppermute | solution.py:10
  21.9 3.7 %dynamic-slice_bitcast_fusion = (bf16[256,1024]{1,0:T(8,128)(2,1)S(1)}, bf16[256,1024]{1,0:T(8,128)(2,1)}, bf16[256,1024]{1,0:T(8,128)(2,1)}, bf16[256,1024]{1,0...) fusion(bf16[4,2,2,256,1024]{4,3,2,1,0:T(8,128)(2,1)} %bitcast.1, ...), kind=kLoop, calls=%fused_computation.32 | loop fusion | bytes 8388636 | tf_op jit(solution)/shard_map/reshape | solution.py:72
  25.6 5.5 %collective-permute-done.4 = bf16[80,1024]{1,0:T(8,128)(2,1)S(1)} collective-permute-done((bf16[80,1024]{1,0:T(8,128)(2,1)S(1)}, bf16[80,1024]{1,0:T(8,128)(2,1)S(1)}, u32[]{:S(2)}, u32[]{:S(2)}) %collective-permute-start.4) | collective-permute-done | bytes 163872 | tf_op jit(solution)/shard_map/ppermute | solution.py:10
  31.1 0.7 copy-done.11
  31.7 0.9 %pad_maximum_fusion = bf16[320,1024]{1,0:T(8,128)(2,1)} fusion(bf16[80,1024]{1,0:T(8,128)(2,1)S(1)} %collective-permute-done.5, bf16[80,1024]{1,0:T(8,128)(2,1)S(1)} %collective-permute-done.4, bf16[80,1024]{1,0:T(8,128)(2,1)S(1)} %collective-permute-done.3, bf16[80,1024]{1,0:T(8,128)(2,1)S(1)} %maximum_select_fusion.2), kind=kLoop, calls=%fused_computation.31 | loop fusion | flops 2621440 | bytes 1310720 | tf_op jit(solution)/shard_map/concatenate | solution.py:116
  32.6 2.4 %collective-permute-start.6 = (bf16[320,1024]{1,0:T(8,128)(2,1)}, bf16[320,1024]{1,0:T(8,128)(2,1)S(1)}, u32[]{:S(2)}, u32[]{:S(2)}) collective-permute-start(bf16[320,1024]{1,0:T(8,128)(2,1)} %pad_maximum_fusion), channel_id=1, source_target_pairs={{0,16},{16,0},{1,17},{17,1},{2,18},{18,2},{3,19},{19,3},{4,20},{20... | collective-permute-start | bytes 1966088 | tf_op jit(solution)/shard_map/ppermute | solution.py:10
  35.0 1.2 %pad_maximum_fusion.2 = (bf16[160,1024]{1,0:T(8,128)(2,1)S(1)}, bf16[160,1024]{1,0:T(8,128)(2,1)S(1)}) fusion(bf16[80,1024]{1,0:T(8,128)(2,1)} %copy-done.13, bf16[80,1024]{1,0:T(8,128)(2,1)} %copy-done.11, bf16[80,1024]{1,0:T(8,128)(2,1)S(1)} %collective-permute-done.3), kind=kLoop, calls=%fused_computation.49 | loop fusion | flops 1310720 | bytes 1146880 | tf_op jit(solution)/shard_map/concatenate | solution.py:115
  36.2 0.5 collective-permute-start.8
  36.8 1.0 %collective-permute-start.9 = (bf16[160,1024]{1,0:T(8,128)(2,1)S(1)}, bf16[160,1024]{1,0:T(8,128)(2,1)S(1)}, u32[]{:S(2)}, u32[]{:S(2)}) collective-permute-start(bf16[160,1024]{1,0:T(8,128)(2,1)S(1)} %get-tuple-element.69), channel_id=1, source_target_pairs={{0,1},{1,2},{2,3},{3,4},{4,5},{5,6},{6,7},{7,0},{8,9},{9,10},{10,1... | collective-permute-start | bytes 983048 | tf_op jit(solution)/shard_map/ppermute | solution.py:10
  38.2 0.4 fusion
  38.6 2.9 %collective-permute-start.7 = (bf16[320,256]{1,0:T(8,128)(2,1)S(1)}, bf16[320,256]{1,0:T(8,128)(2,1)S(1)}, u32[]{:S(2)}, u32[]{:S(2)}) collective-permute-start(bf16[320,256]{1,0:T(8,128)(2,1)S(1)} %fusion), channel_id=1, source_target_pairs={{0,160},{32,128},{64,224},{96,192},{128,32},{160,0},{192,96},{224,... | collective-permute-start | bytes 491528 | tf_op jit(solution)/shard_map/ppermute | solution.py:80
  42.0 0.4 fusion.6
  42.3 0.9 %collective-permute-start.15 = (bf16[320,256]{1,0:T(8,128)(2,1)S(1)}, bf16[320,256]{1,0:T(8,128)(2,1)S(1)}, u32[]{:S(2)}, u32[]{:S(2)}) collective-permute-start(bf16[320,256]{1,0:T(8,128)(2,1)S(1)} %fusion.6), channel_id=1, source_target_pairs={{0,192},{32,224},{64,0},{96,32},{128,64},{160,96},{192,128},{224,1... | collective-permute-start | bytes 491528 | tf_op jit(solution)/shard_map/ppermute | solution.py:80
  43.7 0.4 fusion.5
  44.1 0.9 %collective-permute-start.14 = (bf16[320,256]{1,0:T(8,128)(2,1)S(1)}, bf16[320,256]{1,0:T(8,128)(2,1)S(1)}, u32[]{:S(2)}, u32[]{:S(2)}) collective-permute-start(bf16[320,256]{1,0:T(8,128)(2,1)S(1)} %fusion.5), channel_id=1, source_target_pairs={{0,64},{32,96},{64,128},{96,160},{128,192},{160,224},{192,0},{224,... | collective-permute-start | bytes 491528 | tf_op jit(solution)/shard_map/ppermute | solution.py:80
  45.3 0.4 fusion.25
  45.7 0.4 fusion.24
  46.1 0.4 fusion.23
  46.7 0.4 fusion.4
  47.1 0.7 copy-done.7
  47.8 0.4 fusion.3
  48.2 0.7 copy-done.6
  48.8 0.4 fusion.2
  49.2 1.2 %collective-permute-start.13 = (bf16[320,256]{1,0:T(8,128)(2,1)S(1)}, bf16[320,256]{1,0:T(8,128)(2,1)S(1)}, u32[]{:S(2)}, u32[]{:S(2)}) collective-permute-start(bf16[320,256]{1,0:T(8,128)(2,1)S(1)} %fusion.4), channel_id=1, source_target_pairs={{0,32},{32,0},{64,96},{96,64},{128,160},{160,128},{192,224},{224,1... | collective-permute-start | bytes 491528 | tf_op jit(solution)/shard_map/ppermute | solution.py:80
  50.4 1.2 %collective-permute-start.12 = (bf16[320,256]{1,0:T(8,128)(2,1)S(1)}, bf16[320,256]{1,0:T(8,128)(2,1)S(1)}, u32[]{:S(2)}, u32[]{:S(2)}) collective-permute-start(bf16[320,256]{1,0:T(8,128)(2,1)S(1)} %fusion.3), channel_id=1, source_target_pairs={{0,128},{32,160},{64,192},{96,224},{128,0},{160,32},{192,64},{224,... | collective-permute-start | bytes 491528 | tf_op jit(solution)/shard_map/ppermute | solution.py:80
  51.6 1.8 %collective-permute-start.16 = (bf16[320,1024]{1,0:T(8,128)(2,1)S(1)}, bf16[320,1024]{1,0:T(8,128)(2,1)S(1)}, u32[]{:S(2)}, u32[]{:S(2)}) collective-permute-start(bf16[320,1024]{1,0:T(8,128)(2,1)S(1)} %constant_dynamic-update-slice_fusion), channel_id=1, source_target_pairs={{0,16},{16,0},{1,17},{17,1},{2,18},{18,2},{3,19},{19,3},{4,20},{20... | collective-permute-start | bytes 1966088 | tf_op jit(solution)/shard_map/ppermute | solution.py:10
  53.4 0.4 fusion.1
  53.8 0.4 fusion.21
  54.2 0.7 copy-done.3
  54.8 0.4 convolution_add_fusion.15.refs_1_
  55.2 2.0 %collective-permute-start.11 = (bf16[320,256]{1,0:T(8,128)(2,1)S(1)}, bf16[320,256]{1,0:T(8,128)(2,1)S(1)}, u32[]{:S(2)}, u32[]{:S(2)}) collective-permute-start(bf16[320,256]{1,0:T(8,128)(2,1)S(1)} %fusion.2), channel_id=1, source_target_pairs={{0,224},{32,192},{64,32},{96,0},{128,96},{160,64},{192,160},{224,1... | collective-permute-start | bytes 491528 | tf_op jit(solution)/shard_map/ppermute | solution.py:80
  57.6 0.4 fusion.13
  58.0 0.4 fusion.35
  58.3 0.4 fusion.12
  58.7 0.4 fusion.34
  59.1 0.4 fusion.11
  59.5 0.4 fusion.33
  59.9 0.4 fusion.10
  60.2 0.4 fusion.32
  60.6 0.4 fusion.9
  61.0 0.4 fusion.31
  61.4 0.4 fusion.8
  61.8 0.4 fusion.30
  62.1 0.4 fusion.7
  62.5 0.5 collective-permute-start.10
  63.1 3.0 %collective-permute-start.23 = (bf16[320,256]{1,0:T(8,128)(2,1)S(1)}, bf16[320,256]{1,0:T(8,128)(2,1)S(1)}, u32[]{:S(2)}, u32[]{:S(2)}) collective-permute-start(bf16[320,256]{1,0:T(8,128)(2,1)S(1)} %fusion.13), channel_id=1, source_target_pairs={{0,192},{32,224},{64,0},{96,32},{128,64},{160,96},{192,128},{224,1... | collective-permute-start | bytes 491528 | tf_op jit(solution)/shard_map/ppermute | solution.py:80
  66.5 0.7 collective-permute-start.21
  67.2 1.3 %collective-permute-start.20 = (bf16[320,256]{1,0:T(8,128)(2,1)S(1)}, bf16[320,256]{1,0:T(8,128)(2,1)S(1)}, u32[]{:S(2)}, u32[]{:S(2)}) collective-permute-start(bf16[320,256]{1,0:T(8,128)(2,1)S(1)} %fusion.10), channel_id=1, source_target_pairs={{0,128},{32,160},{64,192},{96,224},{128,0},{160,32},{192,64},{224,... | collective-permute-start | bytes 491528 | tf_op jit(solution)/shard_map/ppermute | solution.py:80
  68.4 1.6 %collective-permute-done.10.refs_3_ = bf16[320,256]{1,0:T(8,128)(2,1)S(1)} collective-permute-done((bf16[320,256]{1,0:T(8,128)(2,1)S(1)}, bf16[320,256]{1,0:T(8,128)(2,1)S(1)}, u32[]{:S(2)}, u32[]{:S(2)}) %collective-permute-start.10) | collective-permute-done | bytes 163872 | tf_op jit(solution)/shard_map/ppermute | solution.py:80
  70.0 0.7 collective-permute-start.19
  70.7 1.6 %collective-permute-start.18 = (bf16[320,256]{1,0:T(8,128)(2,1)S(1)}, bf16[320,256]{1,0:T(8,128)(2,1)S(1)}, u32[]{:S(2)}, u32[]{:S(2)}) collective-permute-start(bf16[320,256]{1,0:T(8,128)(2,1)S(1)} %fusion.8), channel_id=1, source_target_pairs={{0,96},{32,64},{64,160},{96,128},{128,224},{160,192},{192,32},{224... | collective-permute-start | bytes 491528 | tf_op jit(solution)/shard_map/ppermute | solution.py:80
  72.4 3.9 %collective-permute-done.22.refs_15_ = bf16[320,256]{1,0:T(8,128)(2,1)S(1)} collective-permute-done((bf16[320,256]{1,0:T(8,128)(2,1)S(1)}, bf16[320,256]{1,0:T(8,128)(2,1)S(1)}, u32[]{:S(2)}, u32[]{:S(2)}) %collective-permute-start.22) | collective-permute-done | bytes 163872 | tf_op jit(solution)/shard_map/ppermute | solution.py:80
  76.3 0.4 convolution_add_fusion.7.refs_9_
  76.7 1.0 %collective-permute-done.19.refs_12_ = bf16[320,256]{1,0:T(8,128)(2,1)S(1)} collective-permute-done((bf16[320,256]{1,0:T(8,128)(2,1)S(1)}, bf16[320,256]{1,0:T(8,128)(2,1)S(1)}, u32[]{:S(2)}, u32[]{:S(2)}) %collective-permute-start.19) | collective-permute-done | bytes 163872 | tf_op jit(solution)/shard_map/ppermute | solution.py:80
  77.7 3.7 %collective-permute-done.18.refs_11_ = bf16[320,256]{1,0:T(8,128)(2,1)S(1)} collective-permute-done((bf16[320,256]{1,0:T(8,128)(2,1)S(1)}, bf16[320,256]{1,0:T(8,128)(2,1)S(1)}, u32[]{:S(2)}, u32[]{:S(2)}) %collective-permute-start.18) | collective-permute-done | bytes 163872 | tf_op jit(solution)/shard_map/ppermute | solution.py:80
  81.4 2.9 %collective-permute-done.17.refs_10_ = bf16[320,256]{1,0:T(8,128)(2,1)S(1)} collective-permute-done((bf16[320,256]{1,0:T(8,128)(2,1)S(1)}, bf16[320,256]{1,0:T(8,128)(2,1)S(1)}, u32[]{:S(2)}, u32[]{:S(2)}) %collective-permute-start.17) | collective-permute-done | bytes 163872 | tf_op jit(solution)/shard_map/ppermute | solution.py:80
  84.4 1.4 %total_scores.1 = f32[256,640]{1,0:T(8,128)} custom-call(s32[1]{0:T(128)} %bitcast.refs_0_, f32[320,256]{1,0:T(8,128)S(1)} %convolution_add_fusion.15.refs_1_, bf16[320,256]{1,0:T(8,128)(2,1)S(1)} %collective-permute-done.7.refs_2_, bf16[320,256]{1,0:T(8,128)(2,1)S(1)} %collective-permute-done.10.refs_3_, ...), custom_call_target="tpu_custom_call" | custom-call | flops 1310720 | bytes 3276800 | tf_op jit(solution)/shard_map/total_scores/pallas_call | solution.py:42
  (59 shorter events, 3.0 us)
Async XLA Ops:
  0.0 4.4 %collective-permute-start = (bf16[40,1024]{1,0:T(8,128)(2,1)}, bf16[40,1024]{1,0:T(8,128)(2,1)S(1)}, u32[]{:S(2)}, u32[]{:S(2)}) collective-permute-start(bf16[40,1024]{1,0:T(8,128)(2,1)} %param.4), channel_id=1, source_target_pairs={{0,16},{16,0},{1,17},{17,1},{2,18},{18,2},{3,19},{19,3},{4,20},{20... | collective-permute-start | bytes 245768 | tf_op jit(solution)/shard_map/ppermute | solution.py:10
  4.4 17.5 %collective-permute-start.2 = (bf16[4096,1024]{1,0:T(8,128)(2,1)}, bf16[4096,1024]{1,0:T(8,128)(2,1)}, u32[]{:S(2)}, u32[]{:S(2)}) collective-permute-start(bf16[4096,1024]{1,0:T(8,128)(2,1)} %param.3), channel_id=1, source_target_pairs={{0,16},{16,0},{1,17},{17,1},{2,18},{18,2},{3,19},{19,3},{4,20},{20... | collective-permute-start | bytes 25165832 | tf_op jit(solution)/shard_map/ppermute | solution.py:10
  7.8 5.5 %collective-permute-start.1 = (bf16[40,1024]{1,0:T(8,128)(2,1)S(1)}, bf16[40,1024]{1,0:T(8,128)(2,1)S(1)}, u32[]{:S(2)}, u32[]{:S(2)}) collective-permute-start(bf16[40,1024]{1,0:T(8,128)(2,1)S(1)} %convolution_convert_fusion), channel_id=1, source_target_pairs={{0,8},{8,0},{1,9},{9,1},{2,10},{10,2},{3,11},{11,3},{4,12},{12,4},... | collective-permute-start | bytes 245768 | tf_op jit(solution)/shard_map/ppermute | solution.py:10
  13.4 17.7 %copy-start.15 = (bf16[80,1024]{1,0:T(8,128)(2,1)}, bf16[80,1024]{1,0:T(8,128)(2,1)S(1)}, u32[]{:S(2)}) copy-start(bf16[80,1024]{1,0:T(8,128)(2,1)S(1)} %maximum_select_fusion.2) | copy-start | bytes 491524
  13.4 12.2 %collective-permute-start.3 = (bf16[80,1024]{1,0:T(8,128)(2,1)S(1)}, bf16[80,1024]{1,0:T(8,128)(2,1)S(1)}, u32[]{:S(2)}, u32[]{:S(2)}) collective-permute-start(bf16[80,1024]{1,0:T(8,128)(2,1)S(1)} %maximum_select_fusion.2), channel_id=1, source_target_pairs={{0,7},{1,0},{2,1},{3,2},{4,3},{5,4},{6,5},{7,6},{8,15},{9,8},{10,9... | collective-permute-start | bytes 491528 | tf_op jit(solution)/shard_map/ppermute | solution.py:10
  19.1 12.0 %collective-permute-start.4 = (bf16[80,1024]{1,0:T(8,128)(2,1)S(1)}, bf16[80,1024]{1,0:T(8,128)(2,1)S(1)}, u32[]{:S(2)}, u32[]{:S(2)}) collective-permute-start(bf16[80,1024]{1,0:T(8,128)(2,1)S(1)} %maximum_select_fusion.2), channel_id=1, source_target_pairs={{0,4},{1,5},{2,6},{3,7},{4,0},{5,1},{6,2},{7,3},{8,12},{9,13},{10,... | collective-permute-start | bytes 491528 | tf_op jit(solution)/shard_map/ppermute | solution.py:10
  20.5 10.6 %collective-permute-start.5 = (bf16[80,1024]{1,0:T(8,128)(2,1)S(1)}, bf16[80,1024]{1,0:T(8,128)(2,1)S(1)}, u32[]{:S(2)}, u32[]{:S(2)}) collective-permute-start(bf16[80,1024]{1,0:T(8,128)(2,1)S(1)} %maximum_select_fusion.2), channel_id=1, source_target_pairs={{0,1},{1,2},{2,3},{3,4},{4,5},{5,6},{6,7},{7,0},{8,9},{9,10},{10,1... | collective-permute-start | bytes 491528 | tf_op jit(solution)/shard_map/ppermute | solution.py:10
  31.0 0.7 copy-start.11
  31.7 0.9 %copy-start.13 = (bf16[80,1024]{1,0:T(8,128)(2,1)}, bf16[80,1024]{1,0:T(8,128)(2,1)S(1)}, u32[]{:S(2)}) copy-start(bf16[80,1024]{1,0:T(8,128)(2,1)S(1)} %collective-permute-done.5) | copy-start | bytes 491524
  32.6 5.2 %collective-permute-start.6 = (bf16[320,1024]{1,0:T(8,128)(2,1)}, bf16[320,1024]{1,0:T(8,128)(2,1)S(1)}, u32[]{:S(2)}, u32[]{:S(2)}) collective-permute-start(bf16[320,1024]{1,0:T(8,128)(2,1)} %pad_maximum_fusion), channel_id=1, source_target_pairs={{0,16},{16,0},{1,17},{17,1},{2,18},{18,2},{3,19},{19,3},{4,20},{20... | collective-permute-start | bytes 1966088 | tf_op jit(solution)/shard_map/ppermute | solution.py:10
  35.0 3.1 %copy-start.4 = (bf16[256,1024]{1,0:T(8,128)(2,1)S(1)}, bf16[256,1024]{1,0:T(8,128)(2,1)}, u32[]{:S(2)}) copy-start(bf16[256,1024]{1,0:T(8,128)(2,1)} %get-tuple-element.36) | copy-start | bytes 1572868
  35.0 3.2 %copy-start.12 = (bf16[80,1024]{1,0:T(8,128)(2,1)S(1)}, bf16[80,1024]{1,0:T(8,128)(2,1)}, u32[]{:S(2)}) copy-start(bf16[80,1024]{1,0:T(8,128)(2,1)} %copy-done.11) | copy-start | bytes 491524
  35.0 3.2 %copy-start.14 = (bf16[80,1024]{1,0:T(8,128)(2,1)S(1)}, bf16[80,1024]{1,0:T(8,128)(2,1)}, u32[]{:S(2)}) copy-start(bf16[80,1024]{1,0:T(8,128)(2,1)} %copy-done.13) | copy-start | bytes 491524
  35.0 3.2 %copy-start.16 = (bf16[80,1024]{1,0:T(8,128)(2,1)S(1)}, bf16[80,1024]{1,0:T(8,128)(2,1)}, u32[]{:S(2)}) copy-start(bf16[80,1024]{1,0:T(8,128)(2,1)} %copy-done.15) | copy-start | bytes 491524
  36.2 13.0 %collective-permute-start.8 = (bf16[160,1024]{1,0:T(8,128)(2,1)S(1)}, bf16[160,1024]{1,0:T(8,128)(2,1)S(1)}, u32[]{:S(2)}, u32[]{:S(2)}) collective-permute-start(bf16[160,1024]{1,0:T(8,128)(2,1)S(1)} %get-tuple-element.70), channel_id=1, source_target_pairs={{0,7},{1,0},{2,1},{3,2},{4,3},{5,4},{6,5},{7,6},{8,15},{9,8},{10,9... | collective-permute-start | bytes 983048 | tf_op jit(solution)/shard_map/ppermute | solution.py:10
  36.8 13.6 %collective-permute-start.9 = (bf16[160,1024]{1,0:T(8,128)(2,1)S(1)}, bf16[160,1024]{1,0:T(8,128)(2,1)S(1)}, u32[]{:S(2)}, u32[]{:S(2)}) collective-permute-start(bf16[160,1024]{1,0:T(8,128)(2,1)S(1)} %get-tuple-element.69), channel_id=1, source_target_pairs={{0,1},{1,2},{2,3},{3,4},{4,5},{5,6},{6,7},{7,0},{8,9},{9,10},{10,1... | collective-permute-start | bytes 983048 | tf_op jit(solution)/shard_map/ppermute | solution.py:10
  38.2 3.3 %copy-start.2 = (bf16[256,1024]{1,0:T(8,128)(2,1)S(1)}, bf16[256,1024]{1,0:T(8,128)(2,1)}, u32[]{:S(2)}) copy-start(bf16[256,1024]{1,0:T(8,128)(2,1)} %get-tuple-element.50) | copy-start | bytes 1572868
  38.6 3.3 %copy-start.10 = (bf16[256,1024]{1,0:T(8,128)(2,1)S(1)}, bf16[256,1024]{1,0:T(8,128)(2,1)}, u32[]{:S(2)}) copy-start(bf16[256,1024]{1,0:T(8,128)(2,1)} %get-tuple-element.49) | copy-start | bytes 1572868
  38.6 12.9 %collective-permute-start.7 = (bf16[320,256]{1,0:T(8,128)(2,1)S(1)}, bf16[320,256]{1,0:T(8,128)(2,1)S(1)}, u32[]{:S(2)}, u32[]{:S(2)}) collective-permute-start(bf16[320,256]{1,0:T(8,128)(2,1)S(1)} %fusion), channel_id=1, source_target_pairs={{0,160},{32,128},{64,224},{96,192},{128,32},{160,0},{192,96},{224,... | collective-permute-start | bytes 491528 | tf_op jit(solution)/shard_map/ppermute | solution.py:80
  41.9 1.3 %copy-start.1 = (bf16[256,1024]{1,0:T(8,128)(2,1)S(1)}, bf16[256,1024]{1,0:T(8,128)(2,1)}, u32[]{:S(2)}) copy-start(bf16[256,1024]{1,0:T(8,128)(2,1)} %get-tuple-element.48) | copy-start | bytes 1572868
  42.3 1.3 %copy-start.9 = (bf16[256,1024]{1,0:T(8,128)(2,1)S(1)}, bf16[256,1024]{1,0:T(8,128)(2,1)}, u32[]{:S(2)}) copy-start(bf16[256,1024]{1,0:T(8,128)(2,1)} %get-tuple-element.47) | copy-start | bytes 1572868
  42.3 20.2 %collective-permute-start.15 = (bf16[320,256]{1,0:T(8,128)(2,1)S(1)}, bf16[320,256]{1,0:T(8,128)(2,1)S(1)}, u32[]{:S(2)}, u32[]{:S(2)}) collective-permute-start(bf16[320,256]{1,0:T(8,128)(2,1)S(1)} %fusion.6), channel_id=1, source_target_pairs={{0,192},{32,224},{64,0},{96,32},{128,64},{160,96},{192,128},{224,1... | collective-permute-start | bytes 491528 | tf_op jit(solution)/shard_map/ppermute | solution.py:80
  43.7 1.3 %copy-start = (bf16[256,1024]{1,0:T(8,128)(2,1)S(1)}, bf16[256,1024]{1,0:T(8,128)(2,1)}, u32[]{:S(2)}) copy-start(bf16[256,1024]{1,0:T(8,128)(2,1)} %get-tuple-element.46) | copy-start | bytes 1572868
  44.1 19.0 %collective-permute-start.14 = (bf16[320,256]{1,0:T(8,128)(2,1)S(1)}, bf16[320,256]{1,0:T(8,128)(2,1)S(1)}, u32[]{:S(2)}, u32[]{:S(2)}) collective-permute-start(bf16[320,256]{1,0:T(8,128)(2,1)S(1)} %fusion.5), channel_id=1, source_target_pairs={{0,64},{32,96},{64,128},{96,160},{128,192},{160,224},{192,0},{224,... | collective-permute-start | bytes 491528 | tf_op jit(solution)/shard_map/ppermute | solution.py:80
  45.7 1.0 %copy-start.8 = (bf16[256,1024]{1,0:T(8,128)(2,1)S(1)}, bf16[256,1024]{1,0:T(8,128)(2,1)}, u32[]{:S(2)}) copy-start(bf16[256,1024]{1,0:T(8,128)(2,1)} %get-tuple-element.45) | copy-start | bytes 1572868
  46.7 1.0 %copy-start.7 = (bf16[256,1024]{1,0:T(8,128)(2,1)S(1)}, bf16[256,1024]{1,0:T(8,128)(2,1)}, u32[]{:S(2)}) copy-start(bf16[256,1024]{1,0:T(8,128)(2,1)} %get-tuple-element.43) | copy-start | bytes 1572868
  47.8 1.0 %copy-start.6 = (bf16[256,1024]{1,0:T(8,128)(2,1)S(1)}, bf16[256,1024]{1,0:T(8,128)(2,1)}, u32[]{:S(2)}) copy-start(bf16[256,1024]{1,0:T(8,128)(2,1)} %get-tuple-element.41) | copy-start | bytes 1572868
  49.2 4.2 %copy-start.5 = (bf16[256,1024]{1,0:T(8,128)(2,1)S(1)}, bf16[256,1024]{1,0:T(8,128)(2,1)}, u32[]{:S(2)}) copy-start(bf16[256,1024]{1,0:T(8,128)(2,1)} %get-tuple-element.39) | copy-start | bytes 1572868
  49.2 16.9 %collective-permute-start.13 = (bf16[320,256]{1,0:T(8,128)(2,1)S(1)}, bf16[320,256]{1,0:T(8,128)(2,1)S(1)}, u32[]{:S(2)}, u32[]{:S(2)}) collective-permute-start(bf16[320,256]{1,0:T(8,128)(2,1)S(1)} %fusion.4), channel_id=1, source_target_pairs={{0,32},{32,0},{64,96},{96,64},{128,160},{160,128},{192,224},{224,1... | collective-permute-start | bytes 491528 | tf_op jit(solution)/shard_map/ppermute | solution.py:80
  50.4 16.1 %collective-permute-start.12 = (bf16[320,256]{1,0:T(8,128)(2,1)S(1)}, bf16[320,256]{1,0:T(8,128)(2,1)S(1)}, u32[]{:S(2)}, u32[]{:S(2)}) collective-permute-start(bf16[320,256]{1,0:T(8,128)(2,1)S(1)} %fusion.3), channel_id=1, source_target_pairs={{0,128},{32,160},{64,192},{96,224},{128,0},{160,32},{192,64},{224,... | collective-permute-start | bytes 491528 | tf_op jit(solution)/shard_map/ppermute | solution.py:80
  51.6 3.6 %collective-permute-start.16 = (bf16[320,1024]{1,0:T(8,128)(2,1)S(1)}, bf16[320,1024]{1,0:T(8,128)(2,1)S(1)}, u32[]{:S(2)}, u32[]{:S(2)}) collective-permute-start(bf16[320,1024]{1,0:T(8,128)(2,1)S(1)} %constant_dynamic-update-slice_fusion), channel_id=1, source_target_pairs={{0,16},{16,0},{1,17},{17,1},{2,18},{18,2},{3,19},{19,3},{4,20},{20... | collective-permute-start | bytes 1966088 | tf_op jit(solution)/shard_map/ppermute | solution.py:10
  53.8 1.0 %copy-start.3 = (bf16[256,1024]{1,0:T(8,128)(2,1)S(1)}, bf16[256,1024]{1,0:T(8,128)(2,1)}, u32[]{:S(2)}) copy-start(bf16[256,1024]{1,0:T(8,128)(2,1)} %get-tuple-element.34) | copy-start | bytes 1572868
  55.2 12.0 %collective-permute-start.11 = (bf16[320,256]{1,0:T(8,128)(2,1)S(1)}, bf16[320,256]{1,0:T(8,128)(2,1)S(1)}, u32[]{:S(2)}, u32[]{:S(2)}) collective-permute-start(bf16[320,256]{1,0:T(8,128)(2,1)S(1)} %fusion.2), channel_id=1, source_target_pairs={{0,224},{32,192},{64,32},{96,0},{128,96},{160,64},{192,160},{224,1... | collective-permute-start | bytes 491528 | tf_op jit(solution)/shard_map/ppermute | solution.py:80
  62.5 7.5 %collective-permute-start.10 = (bf16[320,256]{1,0:T(8,128)(2,1)S(1)}, bf16[320,256]{1,0:T(8,128)(2,1)S(1)}, u32[]{:S(2)}, u32[]{:S(2)}) collective-permute-start(bf16[320,256]{1,0:T(8,128)(2,1)S(1)} %fusion.1), channel_id=1, source_target_pairs={{0,96},{32,64},{64,160},{96,128},{128,224},{160,192},{192,32},{224... | collective-permute-start | bytes 491528 | tf_op jit(solution)/shard_map/ppermute | solution.py:80
  63.1 7.7 %collective-permute-start.23 = (bf16[320,256]{1,0:T(8,128)(2,1)S(1)}, bf16[320,256]{1,0:T(8,128)(2,1)S(1)}, u32[]{:S(2)}, u32[]{:S(2)}) collective-permute-start(bf16[320,256]{1,0:T(8,128)(2,1)S(1)} %fusion.13), channel_id=1, source_target_pairs={{0,192},{32,224},{64,0},{96,32},{128,64},{160,96},{192,128},{224,1... | collective-permute-start | bytes 491528 | tf_op jit(solution)/shard_map/ppermute | solution.py:80
  66.1 10.2 %collective-permute-start.22 = (bf16[320,256]{1,0:T(8,128)(2,1)S(1)}, bf16[320,256]{1,0:T(8,128)(2,1)S(1)}, u32[]{:S(2)}, u32[]{:S(2)}) collective-permute-start(bf16[320,256]{1,0:T(8,128)(2,1)S(1)} %fusion.12), channel_id=1, source_target_pairs={{0,64},{32,96},{64,128},{96,160},{128,192},{160,224},{192,0},{224,... | collective-permute-start | bytes 491528 | tf_op jit(solution)/shard_map/ppermute | solution.py:80
  66.5 10.2 %collective-permute-start.21 = (bf16[320,256]{1,0:T(8,128)(2,1)S(1)}, bf16[320,256]{1,0:T(8,128)(2,1)S(1)}, u32[]{:S(2)}, u32[]{:S(2)}) collective-permute-start(bf16[320,256]{1,0:T(8,128)(2,1)S(1)} %fusion.11), channel_id=1, source_target_pairs={{0,32},{32,0},{64,96},{96,64},{128,160},{160,128},{192,224},{224,1... | collective-permute-start | bytes 491528 | tf_op jit(solution)/shard_map/ppermute | solution.py:80
  67.2 9.5 %collective-permute-start.20 = (bf16[320,256]{1,0:T(8,128)(2,1)S(1)}, bf16[320,256]{1,0:T(8,128)(2,1)S(1)}, u32[]{:S(2)}, u32[]{:S(2)}) collective-permute-start(bf16[320,256]{1,0:T(8,128)(2,1)S(1)} %fusion.10), channel_id=1, source_target_pairs={{0,128},{32,160},{64,192},{96,224},{128,0},{160,32},{192,64},{224,... | collective-permute-start | bytes 491528 | tf_op jit(solution)/shard_map/ppermute | solution.py:80
  70.0 7.7 %collective-permute-start.19 = (bf16[320,256]{1,0:T(8,128)(2,1)S(1)}, bf16[320,256]{1,0:T(8,128)(2,1)S(1)}, u32[]{:S(2)}, u32[]{:S(2)}) collective-permute-start(bf16[320,256]{1,0:T(8,128)(2,1)S(1)} %fusion.9), channel_id=1, source_target_pairs={{0,224},{32,192},{64,32},{96,0},{128,96},{160,64},{192,160},{224,1... | collective-permute-start | bytes 491528 | tf_op jit(solution)/shard_map/ppermute | solution.py:80
  70.7 10.7 %collective-permute-start.18 = (bf16[320,256]{1,0:T(8,128)(2,1)S(1)}, bf16[320,256]{1,0:T(8,128)(2,1)S(1)}, u32[]{:S(2)}, u32[]{:S(2)}) collective-permute-start(bf16[320,256]{1,0:T(8,128)(2,1)S(1)} %fusion.8), channel_id=1, source_target_pairs={{0,96},{32,64},{64,160},{96,128},{128,224},{160,192},{192,32},{224... | collective-permute-start | bytes 491528 | tf_op jit(solution)/shard_map/ppermute | solution.py:80
  76.3 8.1 %collective-permute-start.17 = (bf16[320,256]{1,0:T(8,128)(2,1)S(1)}, bf16[320,256]{1,0:T(8,128)(2,1)S(1)}, u32[]{:S(2)}, u32[]{:S(2)}) collective-permute-start(bf16[320,256]{1,0:T(8,128)(2,1)S(1)} %fusion.7), channel_id=1, source_target_pairs={{0,160},{32,128},{64,224},{96,192},{128,32},{160,0},{192,96},{224,... | collective-permute-start | bytes 491528 | tf_op jit(solution)/shard_map/ppermute | solution.py:80

commit v2 on v1

v2 whole, which is shorter than its diff:
```python
import jax
import jax.numpy as jnp
from jax import lax
from jax.experimental import pallas as pl
from jax.experimental.pallas import tpu as pltpu
from jax.sharding import Mesh, PartitionSpec as P
def permute(block, axis, target):
    count = lax.axis_size(axis)
    return lax.ppermute(block, axis, [(i, target(i) % count) for i in range(count)])


def scores_against(rows, queries):
    return jnp.einsum("tf,dqf->tdq", rows, queries, preferred_element_type=jnp.float32)


def total_scores_kernel(steps, block, z_ref, *refs):
    part_refs, out_ref, placed_ref = refs[:-2], refs[-2], refs[-1]
    half = len(steps) * block
    for place, step in enumerate(steps):
        total = None
        for first_pair, part_ref in part_refs:
            row = (place - first_pair) * 2 * block
            if 0 <= row < part_ref.shape[1]:
                for chip in range(part_ref.shape[0]):
                    part = part_ref[chip, pl.ds(row, 2 * block), :].astype(jnp.float32)
                    total = part if total is None else total + part
        z = lax.rem(z_ref[0] + step, len(steps))
        for side in range(2):
            first = pl.multiple_of(side * half + z * block, 8)
            placed_ref[pl.ds(first, block), :] = total[side * block : (side + 1) * block]
    out_ref[...] = placed_ref[...].T


def total_scores(z, parts, steps, block):
    owned = parts[0][1].shape[2]
    rows = 2 * block * len(steps)
    firsts = [first for first, _ in parts]
    blocks = [part for _, part in parts]

    def kernel(z_ref, *refs):
        count = len(firsts)
        total_scores_kernel(steps, block, z_ref, *zip(firsts, refs[:count]), *refs[count:])

    return pl.pallas_call(
        kernel,
        grid_spec=pltpu.PrefetchScalarGridSpec(
            num_scalar_prefetch=1,
            grid=(1,),
            in_specs=[pl.BlockSpec(part.shape, lambda i, z_ref: (0, 0, 0)) for part in blocks],
            out_specs=pl.BlockSpec((owned, rows), lambda i, z_ref: (0, 0)),
            scratch_shapes=[pltpu.VMEM((rows, owned), jnp.float32)],
        ),
        out_shape=jax.ShapeDtypeStruct((owned, rows), jnp.float32),
        compiler_params=pltpu.CompilerParams(vmem_limit_bytes=16 * 2**20),
        cost_estimate=pl.CostEstimate(
            flops=8 * rows * owned, bytes_accessed=20 * rows * owned, transcendentals=0
        ),
        name="total_scores",
    )(z, *blocks)


def shards(query_grads, train_grads, precond):
    core, y_hi, z = lax.axis_index("core"), lax.axis_index("y_hi"), lax.axis_index("z")

    def other_core(block):
        return permute(block, "core", lambda i: 1 - i)

    def scored_here(queries):
        by_owner = queries.reshape(count_x * count_y, 2, -1, queries.shape[1])
        return lax.dynamic_index_in_dim(by_owner, core, axis=1, keepdims=False)

    def to_owner(part, step_x, step_y):
        route = []
        for i in range(count_x * count_y):
            to_x, to_y = (i // count_y + step_x) % count_x, (i % count_y + step_y) % count_y
            route.append((i, to_x * count_y + to_y))
        return lax.ppermute(part, ("x", "y_lo"), route)

    def scores_of(rows):
        parts = scores_against(rows, own_q) + scores_against(other_core(rows), mate_q)
        return parts.astype(jnp.bfloat16).transpose(1, 0, 2)

    count_x, count_y = lax.axis_size("x"), lax.axis_size("y_lo")
    x, y_lo = lax.axis_index("x"), lax.axis_index("y_lo")
    owners = [(2, 1), (1, 1), (3, 1), (2, 0), (0, 1), (1, 0), (3, 0), (0, 0)]
    train_mate = other_core(train_grads)
    query_sent, train_mate = lax.optimization_barrier((query_grads, train_mate))
    query_mate = other_core(query_sent)
    train_block = jnp.where(
        core == 1,
        jnp.concatenate([train_mate, train_grads], axis=1),
        jnp.concatenate([train_grads, train_mate], axis=1),
    )
    own = jnp.dot(train_block, precond, preferred_element_type=jnp.float32).astype(jnp.bfloat16)

    far = permute(own, "y_hi", lambda i: 1 - i)
    own_q = scored_here(lax.optimization_barrier((query_grads, own))[0])
    own_q, far = lax.optimization_barrier((own_q, far))
    here = jnp.where(y_hi == 1, jnp.concatenate([far, own]), jnp.concatenate([own, far]))
    ahead1 = permute(here, "z", lambda i: i - 1)
    behind1 = permute(here, "z", lambda i: i + 1)
    across = permute(here, "z", lambda i: i + 4)
    mate_q = scored_here(query_mate)
    mate_q, ahead1 = lax.optimization_barrier((mate_q, ahead1))
    ahead = permute(jnp.concatenate([ahead1, across]), "z", lambda i: i - 1)
    behind = permute(jnp.concatenate([across, behind1]), "z", lambda i: i + 1)
    near = scores_of(jnp.concatenate([here, ahead1, across, behind1]))
    near, ahead, behind = lax.optimization_barrier((near, ahead, behind))
    near = lax.all_to_all(near, ("x", "y_lo"), split_axis=0, concat_axis=0, tiled=True)
    rest = scores_of(jnp.concatenate([ahead, behind]))
    parts = [(0, near)]
    for step_x, step_y in owners:
        owner = (x + step_x) % count_x * count_y + (y_lo + step_y) % count_y
        part = lax.dynamic_slice_in_dim(rest, owner, 1)
        if step_x or step_y:
            part = to_owner(part, step_x, step_y)
        parts.append((4, part))
    steps = (0, 1, 4, 7, 2, 5, 3, 6)
    return total_scores(z.reshape(1), parts, steps, own.shape[0])


def solution(mesh):
    split = Mesh(mesh.devices.reshape(4, 2, 2, 2, 8), ("x", "y_lo", "core", "y_hi", "z"))
    wide, loop = ("x", "y_lo", "core"), ("y_hi", "z")
    return jax.shard_map(
        shards,
        mesh=split,
        in_specs=(P(loop, wide), P(loop, wide), P(None, wide)),
        out_specs=P(loop + wide, None),
        check_vma=False,
    )
```

time: 86.5 us -> 87.1 us (level)
  waiting for transfers between devices: 19.8 us -> 36.8 us
  starting transfers between devices: 36 us -> 30.1 us
  local copies, waits for them, and re-layouts: 11 us -> 5.42 us
  matrix products: 15 us -> 12.9 us
  other arithmetic: 2.12 us -> 0.14 us
    ppermute x10, waiting for transfers between devices: 6.62 us -> 15.8 us  [permute(): lax.ppermute(block, axis, [(i, target(i) % count) for i in range(count)])]
    ppermute x14 -> x7, starting transfers between devices: 16.9 us -> 8.57 us  [to_owner(): return lax.ppermute(part, ('x', 'y_lo'), route)]
    reshape x2 -> x0, local copies, waits for them, and re-layouts: 7.95 us -> none  [scored_here(): blocks.append(lax.dynamic_slice(by_owner, start, size).reshape(size[3:]))]
    ppermute x14 -> x7, waiting for transfers between devices: 13.2 us -> 21 us  [to_owner(): return lax.ppermute(part, ('x', 'y_lo'), route)]
    squeeze x0 -> x2, local copies, waits for them, and re-layouts: none -> 5.26 us  [scored_here(): return lax.dynamic_index_in_dim(by_owner, core, axis=1, keepdims=False)]
    all_to_all x0 -> x1, starting transfers between devices: none -> 4.78 us  [shards(): lax.all_to_all(near, ('x', 'y_lo'), split_axis=0, concat_axis=0, tiled=True)]
    unnamed x35 -> x7, local copies, waits for them, and re-layouts: 2.99 us -> 0.03 us
    ppermute x10, starting transfers between devices: 19.1 us -> 16.8 us  [permute(): lax.ppermute(block, axis, [(i, target(i) % count) for i in range(count)])]
  transfers between devices with their start and end apart: 24 -> 18, of which waited for: 7 -> 11; matrix products, arithmetic and copies ran while one was open for 28% -> 21% of each run, Pallas kernels for 0% -> 0%
where the time goes in v2:
time: 87.1 us; the launch traced here: 86.9 us
  waiting for transfers between devices  36.8 us (42%)
  starting transfers between devices  30.1 us (35%)
  matrix products  12.9 us (15%)
  local copies, waits for them, and re-layouts  5.42 us (6%)
  Pallas kernels  1.39 us (2%)
    ppermute x7, waiting for transfers between devices, to_owner(): return lax.ppermute(part, ('x', 'y_lo'), route)  21 us
    ppermute x10, starting transfers between devices, permute(): lax.ppermute(block, axis, [(i, target(i) % count) for i in range(count)])  16.8 us
    ppermute x10, waiting for transfers between devices, permute(): lax.ppermute(block, axis, [(i, target(i) % count) for i in range(count)])  15.8 us
    dot_general x4, matrix products, scores_against(): jnp.einsum('tf,dqf->tdq', rows, queries, preferred_element_type=jnp.float32)  9.76 us
    ppermute x7, starting transfers between devices, to_owner(): return lax.ppermute(part, ('x', 'y_lo'), route)  8.57 us
    squeeze x2, local copies, waits for them, and re-layouts, scored_here(): return lax.dynamic_index_in_dim(by_owner, core, axis=1, keepdims=False)  5.26 us
    all_to_all x1, starting transfers between devices, shards(): lax.all_to_all(near, ('x', 'y_lo'), split_axis=0, concat_axis=0, tiled=True)  4.78 us
    dot_general x1, matrix products, shards(): jnp.dot(train_block, precond, preferred_element_type=jnp.float32)  3.11 us
  transfers between devices with their start and end apart: 18, of which 11 were waited for; matrix products, arithmetic and copies ran while one was open for 21% of the time, Pallas kernels for 0%

profile of v2, /device:TPU:1, one launch (start us, length us, event | category | flops | bytes accessed | tf_op | source)
XLA Modules:
  0.0 86.9 jit_solution(5275550766417752678)
XLA Ops:
  0.0 3.2 %collective-permute-start = (bf16[40,1024]{1,0:T(8,128)(2,1)}, bf16[40,1024]{1,0:T(8,128)(2,1)S(1)}, u32[]{:S(2)}, u32[]{:S(2)}) collective-permute-start(bf16[40,1024]{1,0:T(8,128)(2,1)} %param.4), channel_id=1, source_target_pairs={{0,16},{16,0},{1,17},{17,1},{2,18},{18,2},{3,19},{19,3},{4,20},{20... | collective-permute-start | bytes 245768 | tf_op jit(solution)/shard_map/ppermute | solution.py:9
  3.2 1.1 %collective-permute-done = bf16[40,1024]{1,0:T(8,128)(2,1)S(1)} collective-permute-done((bf16[40,1024]{1,0:T(8,128)(2,1)}, bf16[40,1024]{1,0:T(8,128)(2,1)S(1)}, u32[]{:S(2)}, u32[]{:S(2)}) %collective-permute-start) | collective-permute-done | bytes 81952 | tf_op jit(solution)/shard_map/ppermute | solution.py:9
  4.4 0.4 collective-permute-start.2
  4.7 3.1 %convolution_convert_fusion = bf16[40,1024]{1,0:T(8,128)(2,1)S(1)} fusion(bf16[2048,1024]{1,0:T(8,128)(2,1)} %param.5, bf16[40,1024]{1,0:T(8,128)(2,1)} %param.4, bf16[40,1024]{1,0:T(8,128)(2,1)S(1)} %collective-permute-done, pred[]{:T(512)S(6)} %eq.24), kind=kOutput, calls=%fused_computation.5 | convolution fusion | flops 168550400 | bytes 4440065 | tf_op jit(solution)/shard_map/dot_general | solution.py:94
  7.8 1.3 %collective-permute-start.1 = (bf16[40,1024]{1,0:T(8,128)(2,1)S(1)}, bf16[40,1024]{1,0:T(8,128)(2,1)S(1)}, u32[]{:S(2)}, u32[]{:S(2)}) collective-permute-start(bf16[40,1024]{1,0:T(8,128)(2,1)S(1)} %convolution_convert_fusion), channel_id=1, source_target_pairs={{0,8},{8,0},{1,9},{9,1},{2,10},{10,2},{3,11},{11,3},{4,12},{12,4},... | collective-permute-start | bytes 245768 | tf_op jit(solution)/shard_map/ppermute | solution.py:9
  9.1 2.6 %dynamic-slice_bitcast_fusion.1 = bf16[8,256,1024]{2,1,0:T(8,128)(2,1)S(1)} fusion(bf16[8,2,256,1024]{3,2,1,0:T(8,128)(2,1)} %bitcast.42, s32[]{:T(128)S(6)} %select_n.95), kind=kLoop, calls=%fused_computation.1 | loop fusion | bytes 8388612 | tf_op jit(solution)/shard_map/jit(dynamic_index_in_dim)/squeeze | solution.py:70
  11.7 0.0 copy-start
  11.8 1.6 %collective-permute-done.1 = bf16[40,1024]{1,0:T(8,128)(2,1)S(1)} collective-permute-done((bf16[40,1024]{1,0:T(8,128)(2,1)S(1)}, bf16[40,1024]{1,0:T(8,128)(2,1)S(1)}, u32[]{:S(2)}, u32[]{:S(2)}) %collective-permute-start.1) | collective-permute-done | bytes 81952 | tf_op jit(solution)/shard_map/ppermute | solution.py:9
  13.4 4.1 %collective-permute-start.3 = (bf16[80,1024]{1,0:T(8,128)(2,1)S(1)}, bf16[80,1024]{1,0:T(8,128)(2,1)S(1)}, u32[]{:S(2)}, u32[]{:S(2)}) collective-permute-start(bf16[80,1024]{1,0:T(8,128)(2,1)S(1)} %maximum_select_fusion.2), channel_id=1, source_target_pairs={{0,7},{1,0},{2,1},{3,2},{4,3},{5,4},{6,5},{7,6},{8,15},{9,8},{10,9... | collective-permute-start | bytes 491528 | tf_op jit(solution)/shard_map/ppermute | solution.py:9
  17.5 0.0 collective-permute-start.5
  17.5 2.8 %collective-permute-start.4 = (bf16[80,1024]{1,0:T(8,128)(2,1)S(1)}, bf16[80,1024]{1,0:T(8,128)(2,1)S(1)}, u32[]{:S(2)}, u32[]{:S(2)}) collective-permute-start(bf16[80,1024]{1,0:T(8,128)(2,1)S(1)} %maximum_select_fusion.2), channel_id=1, source_target_pairs={{0,4},{1,5},{2,6},{3,7},{4,0},{5,1},{6,2},{7,3},{8,12},{9,13},{10,... | collective-permute-start | bytes 491528 | tf_op jit(solution)/shard_map/ppermute | solution.py:9
  20.3 0.0 collective-permute-done.2
  20.3 2.6 %dynamic-slice_bitcast_fusion = bf16[8,256,1024]{2,1,0:T(8,128)(2,1)S(1)} fusion(bf16[8,2,256,1024]{3,2,1,0:T(8,128)(2,1)} %bitcast.3, s32[]{:T(128)S(6)} %select_n.95), kind=kLoop, calls=%fused_computation | loop fusion | bytes 8388612 | tf_op jit(solution)/shard_map/jit(dynamic_index_in_dim)/squeeze | solution.py:70
  22.9 0.0 copy-start.2
  22.9 0.0 collective-permute-done.3
  22.9 1.8 %collective-permute-done.5 = bf16[80,1024]{1,0:T(8,128)(2,1)S(1)} collective-permute-done((bf16[80,1024]{1,0:T(8,128)(2,1)S(1)}, bf16[80,1024]{1,0:T(8,128)(2,1)S(1)}, u32[]{:S(2)}, u32[]{:S(2)}) %collective-permute-start.5) | collective-permute-done | bytes 163872 | tf_op jit(solution)/shard_map/ppermute | solution.py:9
  24.8 5.5 %collective-permute-done.4 = bf16[80,1024]{1,0:T(8,128)(2,1)S(1)} collective-permute-done((bf16[80,1024]{1,0:T(8,128)(2,1)S(1)}, bf16[80,1024]{1,0:T(8,128)(2,1)S(1)}, u32[]{:S(2)}, u32[]{:S(2)}) %collective-permute-start.4) | collective-permute-done | bytes 163872 | tf_op jit(solution)/shard_map/ppermute | solution.py:9
  30.3 2.3 %collective-permute-start.6 = (bf16[320,1024]{1,0:T(8,128)(2,1)S(1)}, bf16[320,1024]{1,0:T(8,128)(2,1)S(1)}, u32[]{:S(2)}, u32[]{:S(2)}) collective-permute-start(bf16[320,1024]{1,0:T(8,128)(2,1)S(1)} %pad_maximum_fusion), channel_id=1, source_target_pairs={{0,16},{16,0},{1,17},{17,1},{2,18},{18,2},{3,19},{19,3},{4,20},{20... | collective-permute-start | bytes 1966088 | tf_op jit(solution)/shard_map/ppermute | solution.py:9
  32.6 0.1 pad_maximum_fusion.2
  32.6 1.4 %collective-permute-start.7 = (bf16[160,1024]{1,0:T(8,128)(2,1)S(1)}, bf16[160,1024]{1,0:T(8,128)(2,1)S(1)}, u32[]{:S(2)}, u32[]{:S(2)}) collective-permute-start(bf16[160,1024]{1,0:T(8,128)(2,1)S(1)} %get-tuple-element.34), channel_id=1, source_target_pairs={{0,7},{1,0},{2,1},{3,2},{4,3},{5,4},{6,5},{7,6},{8,15},{9,8},{10,9... | collective-permute-start | bytes 983048 | tf_op jit(solution)/shard_map/ppermute | solution.py:9
  34.0 0.2 collective-permute-start.8
  34.2 0.1 collective-permute-done.6
  34.3 1.6 %fusion.4 = f32[320,8,256]{2,0,1:T(8,128)S(1)} fusion(bf16[8,256,1024]{2,1,0:T(8,128)(2,1)S(1)} %dynamic-slice_bitcast_fusion, bf16[320,1024]{1,0:T(8,128)(2,1)S(1)} %collective-permute-done.6), kind=kOutput, calls=%fused_computation.10 | convolution fusion | flops 1342177280 | bytes 7471104 | tf_op jit(solution)/shard_map/tf,dqf->tdq/dot_general | solution.py:13
  35.9 0.0 copy-done
  35.9 0.0 copy-done.2
  35.9 2.7 %fusion = bf16[8,320,256]{2,1,0:T(8,128)(2,1)} fusion(f32[320,8,256]{2,0,1:T(8,128)S(1)} %fusion.4, bf16[8,256,1024]{2,1,0:T(8,128)(2,1)S(1)} %dynamic-slice_bitcast_fusion.1, bf16[80,1024]{1,0:T(8,128)(2,1)S(1)} %collective-permute-done.5, bf16[80,1024]{1,0:T(8,128)(2,1)S(1)} %collective-permute-done.4, bf16[80,1024]{1,0:T(8,128)(2,1)S(1)} %collective-permute-done.3, ...), kind=kOutput, calls=%fused_computation.4 | convolution fusion | flops 1346109440 | bytes 8781824 | tf_op jit(solution)/shard_map/tf,dqf->tdq/dot_general | solution.py:13
  38.6 3.5 %collective-permute-done.7 = bf16[160,1024]{1,0:T(8,128)(2,1)S(1)} collective-permute-done((bf16[160,1024]{1,0:T(8,128)(2,1)S(1)}, bf16[160,1024]{1,0:T(8,128)(2,1)S(1)}, u32[]{:S(2)}, u32[]{:S(2)}) %collective-permute-start.7) | collective-permute-done | bytes 327712 | tf_op jit(solution)/shard_map/ppermute | solution.py:9
  42.0 2.2 %collective-permute-done.8 = bf16[160,1024]{1,0:T(8,128)(2,1)S(1)} collective-permute-done((bf16[160,1024]{1,0:T(8,128)(2,1)S(1)}, bf16[160,1024]{1,0:T(8,128)(2,1)S(1)}, u32[]{:S(2)}, u32[]{:S(2)}) %collective-permute-start.8) | collective-permute-done | bytes 327712 | tf_op jit(solution)/shard_map/ppermute | solution.py:9
  44.3 1.2 %collective-permute-start.9 = (bf16[320,1024]{1,0:T(8,128)(2,1)S(1)}, bf16[320,1024]{1,0:T(8,128)(2,1)S(1)}, u32[]{:S(2)}, u32[]{:S(2)}) collective-permute-start(bf16[320,1024]{1,0:T(8,128)(2,1)S(1)} %constant_dynamic-update-slice_fusion), channel_id=1, source_target_pairs={{0,16},{16,0},{1,17},{17,1},{2,18},{18,2},{3,19},{19,3},{4,20},{20... | collective-permute-start | bytes 1966088 | tf_op jit(solution)/shard_map/ppermute | solution.py:9
  45.5 4.8 %all-to-all-start = ((bf16[8,320,256]{2,1,0:T(8,128)(2,1)}), bf16[8,320,256]{2,1,0:T(8,128)(2,1)S(1)}, u32[]{:S(2)}, u32[]{:S(2)}) async-start(bf16[8,320,256]{2,1,0:T(8,128)(2,1)} %fusion), calls=%async_computation | async-start | bytes 2621440 | tf_op jit(solution)/shard_map/all_to_all | solution.py:109
  50.2 0.0 copy-start.1
  50.3 0.0 collective-permute-done.9
  50.3 3.9 %fusion.1 = f32[320,8,256]{2,0,1:T(8,128)S(1)} fusion(bf16[8,256,1024]{2,1,0:T(8,128)(2,1)} %copy-done.2, bf16[320,1024]{1,0:T(8,128)(2,1)S(1)} %collective-permute-done.9), kind=kOutput, calls=%fused_computation.7 | convolution fusion | flops 1342177280 | bytes 7471104 | tf_op jit(solution)/shard_map/tf,dqf->tdq/dot_general | solution.py:13
  54.2 0.0 copy-done.1
  54.2 1.6 %add_convert_fusion = bf16[320,8,256]{2,0,1:T(8,128)(2,1)S(1)} fusion(f32[320,8,256]{2,0,1:T(8,128)S(1)} %fusion.1, bf16[8,256,1024]{2,1,0:T(8,128)(2,1)S(1)} %copy-done.1, bf16[320,1024]{1,0:T(8,128)(2,1)S(1)} %constant_dynamic-update-slice_fusion), kind=kOutput, calls=%fused_computation.2 | convolution fusion | flops 1343488000 | bytes 8781824 | tf_op jit(solution)/shard_map/tf,dqf->tdq/dot_general | solution.py:13
  55.8 0.1 dynamic-slice_bitcast_fusion.2
  55.9 3.9 %collective-permute-start.10 = (bf16[1,320,256]{2,1,0:T(8,128)(2,1)S(1)}, bf16[1,320,256]{2,1,0:T(8,128)(2,1)S(1)}, u32[]{:S(2)}, u32[]{:S(2)}) collective-permute-start(bf16[1,320,256]{2,1,0:T(8,128)(2,1)S(1)} %get-tuple-element.32), channel_id=1, source_target_pairs={{0,160},{32,128},{64,224},{96,192},{128,32},{160,0},{192,96},{224,... | collective-permute-start | bytes 491528 | tf_op jit(solution)/shard_map/ppermute | solution.py:77
  59.8 0.3 collective-permute-start.11
  60.1 3.3 %collective-permute-start.12 = (bf16[1,320,256]{2,1,0:T(8,128)(2,1)S(1)}, bf16[1,320,256]{2,1,0:T(8,128)(2,1)S(1)}, u32[]{:S(2)}, u32[]{:S(2)}) collective-permute-start(bf16[1,320,256]{2,1,0:T(8,128)(2,1)S(1)} %get-tuple-element.30), channel_id=1, source_target_pairs={{0,224},{32,192},{64,32},{96,0},{128,96},{160,64},{192,160},{224,1... | collective-permute-start | bytes 491528 | tf_op jit(solution)/shard_map/ppermute | solution.py:77
  63.4 0.0 collective-permute-start.13
  63.4 0.3 collective-permute-start.14
  63.7 11.3 %collective-permute-done.10.refs_1_ = bf16[1,320,256]{2,1,0:T(8,128)(2,1)S(1)} collective-permute-done((bf16[1,320,256]{2,1,0:T(8,128)(2,1)S(1)}, bf16[1,320,256]{2,1,0:T(8,128)(2,1)S(1)}, u32[]{:S(2)}, u32[]{:S(2)}) %collective-permute-start.10) | collective-permute-done | bytes 163872 | tf_op jit(solution)/shard_map/ppermute | solution.py:77
  75.0 0.5 collective-permute-start.15
  75.5 4.2 %collective-permute-done.11.refs_2_ = bf16[1,320,256]{2,1,0:T(8,128)(2,1)S(1)} collective-permute-done((bf16[1,320,256]{2,1,0:T(8,128)(2,1)S(1)}, bf16[1,320,256]{2,1,0:T(8,128)(2,1)S(1)}, u32[]{:S(2)}, u32[]{:S(2)}) %collective-permute-start.11) | collective-permute-done | bytes 163872 | tf_op jit(solution)/shard_map/ppermute | solution.py:77
  79.7 0.3 collective-permute-start.16
  80.0 0.0 collective-permute-done.12.refs_3_
  80.0 3.2 %collective-permute-done.13.refs_4_ = bf16[1,320,256]{2,1,0:T(8,128)(2,1)S(1)} collective-permute-done((bf16[1,320,256]{2,1,0:T(8,128)(2,1)S(1)}, bf16[1,320,256]{2,1,0:T(8,128)(2,1)S(1)}, u32[]{:S(2)}, u32[]{:S(2)}) %collective-permute-start.13) | collective-permute-done | bytes 163872 | tf_op jit(solution)/shard_map/ppermute | solution.py:77
  83.1 0.0 collective-permute-done.14.refs_5_
  83.1 2.3 %collective-permute-done.15.refs_6_ = bf16[1,320,256]{2,1,0:T(8,128)(2,1)S(1)} collective-permute-done((bf16[1,320,256]{2,1,0:T(8,128)(2,1)S(1)}, bf16[1,320,256]{2,1,0:T(8,128)(2,1)S(1)}, u32[]{:S(2)}, u32[]{:S(2)}) %collective-permute-start.15) | collective-permute-done | bytes 163872 | tf_op jit(solution)/shard_map/ppermute | solution.py:77
  85.5 0.0 collective-permute-done.16.refs_7_
  85.5 0.0 all-to-all-done.refs_0_
  85.5 1.4 %total_scores.1 = f32[256,640]{1,0:T(8,128)} custom-call(s32[1]{0:T(128)} %bitcast.z_ref, bf16[8,320,256]{2,1,0:T(8,128)(2,1)S(1)} %all-to-all-done.refs_0_, bf16[1,320,256]{2,1,0:T(8,128)(2,1)S(1)} %collective-permute-done.10.refs_1_, bf16[1,320,256]{2,1,0:T(8,128)(2,1)S(1)} %collective-permute-done.11.refs_2_, ...), custom_call_target="tpu_custom_call" | custom-call | flops 1310720 | bytes 3276800 | tf_op jit(solution)/shard_map/total_scores/pallas_call | solution.py:44
  (4 shorter events, 0.1 us)
Async XLA Ops:
  0.0 4.4 %collective-permute-start = (bf16[40,1024]{1,0:T(8,128)(2,1)}, bf16[40,1024]{1,0:T(8,128)(2,1)S(1)}, u32[]{:S(2)}, u32[]{:S(2)}) collective-permute-start(bf16[40,1024]{1,0:T(8,128)(2,1)} %param.4), channel_id=1, source_target_pairs={{0,16},{16,0},{1,17},{17,1},{2,18},{18,2},{3,19},{19,3},{4,20},{20... | collective-permute-start | bytes 245768 | tf_op jit(solution)/shard_map/ppermute | solution.py:9
  4.4 15.9 %collective-permute-start.2 = (bf16[4096,1024]{1,0:T(8,128)(2,1)}, bf16[4096,1024]{1,0:T(8,128)(2,1)}, u32[]{:S(2)}, u32[]{:S(2)}) collective-permute-start(bf16[4096,1024]{1,0:T(8,128)(2,1)} %param.3), channel_id=1, source_target_pairs={{0,16},{16,0},{1,17},{17,1},{2,18},{18,2},{3,19},{19,3},{4,20},{20... | collective-permute-start | bytes 25165832 | tf_op jit(solution)/shard_map/ppermute | solution.py:9
  7.8 5.5 %collective-permute-start.1 = (bf16[40,1024]{1,0:T(8,128)(2,1)S(1)}, bf16[40,1024]{1,0:T(8,128)(2,1)S(1)}, u32[]{:S(2)}, u32[]{:S(2)}) collective-permute-start(bf16[40,1024]{1,0:T(8,128)(2,1)S(1)} %convolution_convert_fusion), channel_id=1, source_target_pairs={{0,8},{8,0},{1,9},{9,1},{2,10},{10,2},{3,11},{11,3},{4,12},{12,4},... | collective-permute-start | bytes 245768 | tf_op jit(solution)/shard_map/ppermute | solution.py:9
  11.7 24.1 %copy-start = (bf16[8,256,1024]{2,1,0:T(8,128)(2,1)}, bf16[8,256,1024]{2,1,0:T(8,128)(2,1)S(1)}, u32[]{:S(2)}) copy-start(bf16[8,256,1024]{2,1,0:T(8,128)(2,1)S(1)} %dynamic-slice_bitcast_fusion.1) | copy-start | bytes 12582916
  13.4 9.5 %collective-permute-start.3 = (bf16[80,1024]{1,0:T(8,128)(2,1)S(1)}, bf16[80,1024]{1,0:T(8,128)(2,1)S(1)}, u32[]{:S(2)}, u32[]{:S(2)}) collective-permute-start(bf16[80,1024]{1,0:T(8,128)(2,1)S(1)} %maximum_select_fusion.2), channel_id=1, source_target_pairs={{0,7},{1,0},{2,1},{3,2},{4,3},{5,4},{6,5},{7,6},{8,15},{9,8},{10,9... | collective-permute-start | bytes 491528 | tf_op jit(solution)/shard_map/ppermute | solution.py:9
  17.5 7.3 %collective-permute-start.5 = (bf16[80,1024]{1,0:T(8,128)(2,1)S(1)}, bf16[80,1024]{1,0:T(8,128)(2,1)S(1)}, u32[]{:S(2)}, u32[]{:S(2)}) collective-permute-start(bf16[80,1024]{1,0:T(8,128)(2,1)S(1)} %maximum_select_fusion.2), channel_id=1, source_target_pairs={{0,1},{1,2},{2,3},{3,4},{4,5},{5,6},{6,7},{7,0},{8,9},{9,10},{10,1... | collective-permute-start | bytes 491528 | tf_op jit(solution)/shard_map/ppermute | solution.py:9
  17.5 12.8 %collective-permute-start.4 = (bf16[80,1024]{1,0:T(8,128)(2,1)S(1)}, bf16[80,1024]{1,0:T(8,128)(2,1)S(1)}, u32[]{:S(2)}, u32[]{:S(2)}) collective-permute-start(bf16[80,1024]{1,0:T(8,128)(2,1)S(1)} %maximum_select_fusion.2), channel_id=1, source_target_pairs={{0,4},{1,5},{2,6},{3,7},{4,0},{5,1},{6,2},{7,3},{8,12},{9,13},{10,... | collective-permute-start | bytes 491528 | tf_op jit(solution)/shard_map/ppermute | solution.py:9
  22.9 13.0 %copy-start.2 = (bf16[8,256,1024]{2,1,0:T(8,128)(2,1)}, bf16[8,256,1024]{2,1,0:T(8,128)(2,1)S(1)}, u32[]{:S(2)}) copy-start(bf16[8,256,1024]{2,1,0:T(8,128)(2,1)S(1)} %dynamic-slice_bitcast_fusion) | copy-start | bytes 12582916
  30.3 4.0 %collective-permute-start.6 = (bf16[320,1024]{1,0:T(8,128)(2,1)S(1)}, bf16[320,1024]{1,0:T(8,128)(2,1)S(1)}, u32[]{:S(2)}, u32[]{:S(2)}) collective-permute-start(bf16[320,1024]{1,0:T(8,128)(2,1)S(1)} %pad_maximum_fusion), channel_id=1, source_target_pairs={{0,16},{16,0},{1,17},{17,1},{2,18},{18,2},{3,19},{19,3},{4,20},{20... | collective-permute-start | bytes 1966088 | tf_op jit(solution)/shard_map/ppermute | solution.py:9
  32.6 9.4 %collective-permute-start.7 = (bf16[160,1024]{1,0:T(8,128)(2,1)S(1)}, bf16[160,1024]{1,0:T(8,128)(2,1)S(1)}, u32[]{:S(2)}, u32[]{:S(2)}) collective-permute-start(bf16[160,1024]{1,0:T(8,128)(2,1)S(1)} %get-tuple-element.34), channel_id=1, source_target_pairs={{0,7},{1,0},{2,1},{3,2},{4,3},{5,4},{6,5},{7,6},{8,15},{9,8},{10,9... | collective-permute-start | bytes 983048 | tf_op jit(solution)/shard_map/ppermute | solution.py:9
  34.0 10.2 %collective-permute-start.8 = (bf16[160,1024]{1,0:T(8,128)(2,1)S(1)}, bf16[160,1024]{1,0:T(8,128)(2,1)S(1)}, u32[]{:S(2)}, u32[]{:S(2)}) collective-permute-start(bf16[160,1024]{1,0:T(8,128)(2,1)S(1)} %get-tuple-element.33), channel_id=1, source_target_pairs={{0,1},{1,2},{2,3},{3,4},{4,5},{5,6},{6,7},{7,0},{8,9},{9,10},{10,1... | collective-permute-start | bytes 983048 | tf_op jit(solution)/shard_map/ppermute | solution.py:9
  44.3 6.0 %collective-permute-start.9 = (bf16[320,1024]{1,0:T(8,128)(2,1)S(1)}, bf16[320,1024]{1,0:T(8,128)(2,1)S(1)}, u32[]{:S(2)}, u32[]{:S(2)}) collective-permute-start(bf16[320,1024]{1,0:T(8,128)(2,1)S(1)} %constant_dynamic-update-slice_fusion), channel_id=1, source_target_pairs={{0,16},{16,0},{1,17},{17,1},{2,18},{18,2},{3,19},{19,3},{4,20},{20... | collective-permute-start | bytes 1966088 | tf_op jit(solution)/shard_map/ppermute | solution.py:9
  45.5 40.0 %all-to-all-start = ((bf16[8,320,256]{2,1,0:T(8,128)(2,1)}), bf16[8,320,256]{2,1,0:T(8,128)(2,1)S(1)}, u32[]{:S(2)}, u32[]{:S(2)}) async-start(bf16[8,320,256]{2,1,0:T(8,128)(2,1)} %fusion), calls=%async_computation | async-start | bytes 2621440 | tf_op jit(solution)/shard_map/all_to_all | solution.py:109
  50.2 3.9 %copy-start.1 = (bf16[8,256,1024]{2,1,0:T(8,128)(2,1)S(1)}, bf16[8,256,1024]{2,1,0:T(8,128)(2,1)}, u32[]{:S(2)}) copy-start(bf16[8,256,1024]{2,1,0:T(8,128)(2,1)} %copy-done) | copy-start | bytes 12582916
  55.9 19.1 %collective-permute-start.10 = (bf16[1,320,256]{2,1,0:T(8,128)(2,1)S(1)}, bf16[1,320,256]{2,1,0:T(8,128)(2,1)S(1)}, u32[]{:S(2)}, u32[]{:S(2)}) collective-permute-start(bf16[1,320,256]{2,1,0:T(8,128)(2,1)S(1)} %get-tuple-element.32), channel_id=1, source_target_pairs={{0,160},{32,128},{64,224},{96,192},{128,32},{160,0},{192,96},{224,... | collective-permute-start | bytes 491528 | tf_op jit(solution)/shard_map/ppermute | solution.py:77
  59.8 19.8 %collective-permute-start.11 = (bf16[1,320,256]{2,1,0:T(8,128)(2,1)S(1)}, bf16[1,320,256]{2,1,0:T(8,128)(2,1)S(1)}, u32[]{:S(2)}, u32[]{:S(2)}) collective-permute-start(bf16[1,320,256]{2,1,0:T(8,128)(2,1)S(1)} %get-tuple-element.31), channel_id=1, source_target_pairs={{0,96},{32,64},{64,160},{96,128},{128,224},{160,192},{192,32},{224... | collective-permute-start | bytes 491528 | tf_op jit(solution)/shard_map/ppermute | solution.py:77
  60.1 19.8 %collective-permute-start.12 = (bf16[1,320,256]{2,1,0:T(8,128)(2,1)S(1)}, bf16[1,320,256]{2,1,0:T(8,128)(2,1)S(1)}, u32[]{:S(2)}, u32[]{:S(2)}) collective-permute-start(bf16[1,320,256]{2,1,0:T(8,128)(2,1)S(1)} %get-tuple-element.30), channel_id=1, source_target_pairs={{0,224},{32,192},{64,32},{96,0},{128,96},{160,64},{192,160},{224,1... | collective-permute-start | bytes 491528 | tf_op jit(solution)/shard_map/ppermute | solution.py:77
  63.4 19.7 %collective-permute-start.13 = (bf16[1,320,256]{2,1,0:T(8,128)(2,1)S(1)}, bf16[1,320,256]{2,1,0:T(8,128)(2,1)S(1)}, u32[]{:S(2)}, u32[]{:S(2)}) collective-permute-start(bf16[1,320,256]{2,1,0:T(8,128)(2,1)S(1)} %get-tuple-element.29), channel_id=1, source_target_pairs={{0,128},{32,160},{64,192},{96,224},{128,0},{160,32},{192,64},{224,... | collective-permute-start | bytes 491528 | tf_op jit(solution)/shard_map/ppermute | solution.py:77
  63.4 19.7 %collective-permute-start.14 = (bf16[1,320,256]{2,1,0:T(8,128)(2,1)S(1)}, bf16[1,320,256]{2,1,0:T(8,128)(2,1)S(1)}, u32[]{:S(2)}, u32[]{:S(2)}) collective-permute-start(bf16[1,320,256]{2,1,0:T(8,128)(2,1)S(1)} %get-tuple-element.28), channel_id=1, source_target_pairs={{0,32},{32,0},{64,96},{96,64},{128,160},{160,128},{192,224},{224,1... | collective-permute-start | bytes 491528 | tf_op jit(solution)/shard_map/ppermute | solution.py:77
  75.0 10.4 %collective-permute-start.15 = (bf16[1,320,256]{2,1,0:T(8,128)(2,1)S(1)}, bf16[1,320,256]{2,1,0:T(8,128)(2,1)S(1)}, u32[]{:S(2)}, u32[]{:S(2)}) collective-permute-start(bf16[1,320,256]{2,1,0:T(8,128)(2,1)S(1)} %get-tuple-element.27), channel_id=1, source_target_pairs={{0,64},{32,96},{64,128},{96,160},{128,192},{160,224},{192,0},{224,... | collective-permute-start | bytes 491528 | tf_op jit(solution)/shard_map/ppermute | solution.py:77
  79.7 5.8 %collective-permute-start.16 = (bf16[1,320,256]{2,1,0:T(8,128)(2,1)S(1)}, bf16[1,320,256]{2,1,0:T(8,128)(2,1)S(1)}, u32[]{:S(2)}, u32[]{:S(2)}) collective-permute-start(bf16[1,320,256]{2,1,0:T(8,128)(2,1)S(1)} %get-tuple-element.26), channel_id=1, source_target_pairs={{0,192},{32,224},{64,0},{96,32},{128,64},{160,96},{192,128},{224,1... | collective-permute-start | bytes 491528 | tf_op jit(solution)/shard_map/ppermute | solution.py:77
